TPU v7x, 256 devices: a whole 4x4x8 slice. The times are simulated.
256 devices in a mesh: shell: 4 (over z_hi, core), blk: 64 (over z_lo, y, x).
Axes of the slice: x: 4, y: 4, z: 8 (z_hi: 2, z_lo: 4; z = z_hi * 4 + z_lo), core: 2. Of those that a mesh axis runs over, the one named last changes fastest.
Arguments:
- strain_spec: bfloat16 [6, 4, 1024, 2, 1024], P(None, 'shell', 'blk'), may hold values from -6 to 6
- order_map: int32 [1024], replicated, may hold values from 0 to 1023, as said below
- viscosity: float32 [4, 1024, 2048], P('shell', 'blk'), may hold values from 0.2 to 5
- radial_weight: float32 [4], P('shell'), may hold values from 0.3 to 3
Outputs:
- stress_spec: bfloat16 [6, 4, 1024, 2, 1024], P(None, 'shell', 'blk')
- integrated: float32 [6, 1024, 2, 1024], P(None, 'blk', None, 'shell')
Inputs may be any that keep to these rules, and one draw needn't show every extreme that they name: order_map is a permutation of the orders 0 to 1023; the entries 2i and 2i + 1 hold two orders m and 1023 - m, in either order, so each device's 16 slots hold 8 such pairs.
All inputs are finite; a program needn't handle non-finite values.
Results may differ from a plain program's by a relative error of at most 0.014.
Values may be sent and summed in bfloat16 or wider, within the bound.
A program may use at most 128 MiB of HBM per device.

v0:
```python
import math

import jax
import jax.numpy as jnp
from jax import lax
from jax.sharding import PartitionSpec as P

two_power = 1099511627776.0
inverse_power = 1.0 / 1099511627776.0
log_jump = 40.0 * math.log(2.0)


def cycle_geometry(cycle_count):
    cycle_index = jnp.arange(cycle_count // 2, dtype=jnp.float32)
    colatitude = math.pi * (2.0 * cycle_index + 1.0) / (2.0 * cycle_count)
    return (jnp.cos(colatitude), jnp.log(jnp.sin(colatitude)))


def fejer_weights(cycle_count):
    half_count = cycle_count // 2
    cycle_index = jnp.arange(half_count, dtype=jnp.int32)
    wave_number = jnp.arange(1, half_count + 1, dtype=jnp.int32)
    phase_index = wave_number[:, None] * (2 * cycle_index[None, :] + 1) % (2 * cycle_count)
    angles = phase_index.astype(jnp.float32) * (math.pi / cycle_count)
    wave_float = wave_number.astype(jnp.float32)
    divisor = 4.0 * wave_float * wave_float - 1.0
    series = jnp.sum(jnp.cos(angles) / divisor[:, None], axis=0)
    return 2.0 / cycle_count * (1.0 - 2.0 * series)


def legendre_tables(orders, cycle_count, degree_count):
    cosine, log_sine = cycle_geometry(cycle_count)
    order_int = orders[:, None]
    order_float = orders.astype(jnp.float32)[:, None]
    counter = jnp.arange(1, degree_count, dtype=jnp.int32)
    counter_float = counter.astype(jnp.float32)
    factors = jnp.where(
        counter[None, :] <= order_int, jnp.log(1.0 - 0.5 / counter_float)[None, :], 0.0
    )
    log_start = (
        0.5 * jnp.log((2.0 * order_float + 1.0) / (4.0 * math.pi))
        + 0.5 * jnp.sum(factors, axis=1, keepdims=True)
        + order_float * log_sine[None, :]
    )
    even_first = order_int % 2 == 0

    def advance(carry_state, degree):
        previous, latest, log_scale = carry_state
        degree_float = degree.astype(jnp.float32)
        below_float = degree_float - 1.0
        coef_first = jnp.sqrt(
            jnp.maximum(4.0 * degree_float * degree_float - 1.0, 0.0)
            / jnp.maximum(degree_float * degree_float - order_float * order_float, 1.0)
        )
        coef_second = jnp.sqrt(
            jnp.maximum(below_float * below_float - order_float * order_float, 0.0)
            / jnp.maximum(4.0 * below_float * below_float - 1.0, 1.0)
        )
        current = coef_first * (cosine[None, :] * latest - coef_second * previous)
        current = jnp.where(
            degree == order_int + 1,
            jnp.sqrt(2.0 * order_float + 3.0) * cosine[None, :] * latest,
            current,
        )
        current = jnp.where(degree == order_int, 1.0, current)
        current = jnp.where(degree < order_int, 0.0, current)
        result = current * jnp.exp(log_scale)
        too_large = jnp.abs(current) > two_power
        factor = jnp.where(too_large, inverse_power, 1.0)
        next_state = (
            latest * factor,
            current * factor,
            log_scale + jnp.where(too_large, log_jump, 0.0),
        )
        return (next_state, result)

    def pair_step(carry_state, half_degree):
        carry_state, lower_row = advance(carry_state, 2 * half_degree)
        carry_state, upper_row = advance(carry_state, 2 * half_degree + 1)
        even_row = jnp.where(even_first, lower_row, upper_row).astype(jnp.bfloat16)
        odd_row = jnp.where(even_first, upper_row, lower_row).astype(jnp.bfloat16)
        return (carry_state, (even_row, odd_row))

    zero_rows = jnp.zeros((orders.shape[0], cycle_count // 2), jnp.float32)
    initial = (zero_rows, zero_rows, log_start)
    final_state, tables = lax.scan(
        pair_step, initial, jnp.arange(degree_count // 2, dtype=jnp.int32), unroll=32
    )
    return tables


def fourier_table(orders_all, point_count):
    longitudes = jnp.arange(point_count, dtype=jnp.int32)
    phase_index = orders_all[:, None] * longitudes[None, :] % point_count
    angles = phase_index.astype(jnp.float32) * (2.0 * math.pi / point_count)
    return jnp.stack([jnp.cos(angles), -jnp.sin(angles)], axis=1).astype(jnp.bfloat16)


def synthesize(spectra, tables, orders):
    even_first = (orders % 2 == 0)[None, None, :, None, None]
    paired = spectra.reshape(spectra.shape[:-1] + (spectra.shape[-1] // 2, 2))
    even_part = jnp.where(even_first, paired[..., 0], paired[..., 1])
    odd_part = jnp.where(even_first, paired[..., 1], paired[..., 0])
    symmetric = jnp.einsum(
        "csmri,imj->csmrj", even_part, tables[0], preferred_element_type=jnp.float32
    )
    antisymmetric = jnp.einsum(
        "csmri,imj->csmrj", odd_part, tables[1], preferred_element_type=jnp.float32
    )
    north_side = symmetric + antisymmetric
    south_side = symmetric - antisymmetric
    return jnp.concatenate([north_side, jnp.flip(south_side, axis=-1)], axis=-1).astype(
        jnp.bfloat16
    )


def analyze(gridded, tables, orders, weights):
    half_count = gridded.shape[-1] // 2
    north_side = gridded[..., :half_count].astype(jnp.float32)
    south_side = jnp.flip(gridded[..., half_count:], axis=-1).astype(jnp.float32)
    even_side = (weights * (north_side + south_side)).astype(jnp.bfloat16)
    odd_side = (weights * (north_side - south_side)).astype(jnp.bfloat16)
    even_part = jnp.einsum(
        "csmrj,imj->csmri", even_side, tables[0], preferred_element_type=jnp.float32
    )
    odd_part = jnp.einsum(
        "csmrj,imj->csmri", odd_side, tables[1], preferred_element_type=jnp.float32
    )
    even_first = (orders % 2 == 0)[None, None, :, None, None]
    low_side = jnp.where(even_first, even_part, odd_part)
    high_side = jnp.where(even_first, odd_part, even_part)
    stacked = jnp.stack([low_side, high_side], axis=-1)
    return stacked.reshape(stacked.shape[:-2] + (2 * stacked.shape[-2],))


def shards(strain_spec, order_map, viscosity, radial_weight):
    component_count, shell_count, order_count, complex_parts, degree_count = strain_spec.shape
    block_count = lax.axis_size("blk")
    cycle_local = viscosity.shape[1]
    cycle_count = cycle_local * block_count
    point_count = viscosity.shape[2]
    my_orders = lax.dynamic_slice_in_dim(
        order_map, lax.axis_index("blk") * order_count, order_count
    )
    tables = legendre_tables(my_orders, cycle_count, degree_count)
    weights = fejer_weights(cycle_count)
    wave_table = fourier_table(order_map, point_count).reshape(
        block_count, order_count, 2, point_count
    )
    doubling = (
        jnp.where(order_map == 0, 1.0, 2.0).astype(jnp.bfloat16).reshape(block_count, order_count)
    )
    norm_factor = 2.0 * math.pi / point_count
    gridded = synthesize(strain_spec, tables, my_orders)
    item_count = gridded.shape[0]
    pieces = gridded.reshape(item_count, shell_count, order_count, 2, block_count, cycle_local)
    outgoing = pieces.transpose(0, 1, 4, 2, 3, 5).reshape(
        item_count, shell_count, block_count, order_count * 2 * cycle_local
    )
    returns = []
    for component in range(component_count):
        received = lax.all_to_all(
            outgoing[component : component + 1], "blk", split_axis=2, concat_axis=2, tiled=True
        )
        cycle_item_count = received.shape[0]
        blocks = received.reshape(
            cycle_item_count, shell_count, block_count, order_count, 2, cycle_local
        )
        blocks = blocks * doubling[None, None, :, :, None, None]
        grid_field = jnp.einsum(
            "csdxrj,dxrk->csjk", blocks, wave_table, preferred_element_type=jnp.float32
        )
        stress = (viscosity[None] * grid_field).astype(jnp.bfloat16)
        spectra = jnp.einsum(
            "csjk,dxrk->csdxrj", stress, wave_table, preferred_element_type=jnp.float32
        )
        spectra = (spectra * norm_factor).astype(jnp.bfloat16)
        returns.append(
            lax.all_to_all(
                spectra.reshape(
                    cycle_item_count, shell_count, block_count, order_count * 2 * cycle_local
                ),
                "blk",
                split_axis=2,
                concat_axis=2,
                tiled=True,
            )
        )
    returned = jnp.concatenate(returns, axis=0)
    item_count = returned.shape[0]
    pieces = returned.reshape(item_count, shell_count, block_count, order_count, 2, cycle_local)
    coefficient = analyze(
        pieces.transpose(0, 1, 3, 4, 2, 5).reshape(
            item_count, shell_count, order_count, 2, cycle_count
        ),
        tables,
        my_orders,
        weights,
    )
    stress_spec = coefficient.astype(jnp.bfloat16)
    weighted = jnp.sum(coefficient * radial_weight[None, :, None, None, None], axis=1)
    summed = lax.psum(weighted.astype(jnp.bfloat16), "shell").astype(jnp.float32)
    share_size = degree_count // lax.axis_size("shell")
    integrated = lax.dynamic_slice_in_dim(
        summed, lax.axis_index("shell") * share_size, share_size, 3
    )
    return (stress_spec, integrated)


def solution(mesh):
    return jax.shard_map(
        shards,
        mesh=mesh,
        in_specs=(P(None, "shell", "blk", None, None), P(), P("shell", "blk", None), P("shell")),
        out_specs=(P(None, "shell", "blk", None, None), P(None, "blk", None, "shell")),
        check_vma=False,
    )
```

profile of v0, /device:TPU:97, one launch (start us, length us, event | category | flops | bytes accessed | tf_op | source)
XLA Modules:
  0.0 956.6 jit_solution(11079613722453055264)
XLA Ops:
  8.4 453.0 %while.23 = (s32[]{:T(128)}, f32[16,512]{1,0:T(8,128)S(1)}, f32[16,512]{1,0:T(8,128)S(1)}, f32[16,512]{1,0:T(8,128)S(1)}, bf16[16,32,16,512]{3,2,1,0:T(8,128)(2,...) while((s32[]{:T(128)}, f32[16,512]{1,0:T(8,128)S(1)}, ...), condition=%wide.region_2.3_spmd.clone.clone, body=%wide.region_1.2_spmd.clone.clone.sunk | while | flops 11857313 | bytes 9983139 | solution.py:86
  462.9 6.0 fusion.637
  468.8 6.5 copy.243
  475.3 6.6 copy.244
  482.1 12.5 %fusion.457 = f32[16,512,6,2]{1,2,3,0:T(8,128)S(1)} fusion(bf16[512,16,512,1]{2,1,0,3:T(8,128)(2,1)} %bitcast.1497, bf16[6,16,2,512]{3,1,2,0:T(8,128)(2,1)S(1)} %get-tuple-element.1382), kind=kOutput, calls=%fused_computation.1301 | convolution fusion | flops 100663296 | bytes 8978432 | tf_op jit(solution)/shard_map/csmri,imj->csmrj/dot_general | solution.py:107
  494.6 9.2 fusion.459
  511.9 10.4 %all-to-all-start = ((bf16[64,2,256]{2,1,0:T(2,128)(2,1)}), bf16[64,2,256]{2,1,0:T(2,128)(2,1)S(1)}, u32[]{:S(2)}, u32[]{:S(2)}) async-start(bf16[64,2,256]{2,1,0:T(2,128)(2,1)} %reshape.4644), calls=%async_computation | async-start | bytes 131072 | tf_op jit(solution)/shard_map/all_to_all | solution.py:162
  528.8 7.4 all-to-all-start.2
  536.2 37.1 %cosine_convert_fusion = (bf16[64,16,1,2048]{3,0,1,2:T(8,128)(2,1)}, bf16[64,16,1,2048]{3,0,1,2:T(8,128)(2,1)}) fusion(s32[64,16]{0,1:T(8,128)S(1)} %copy.241), kind=kLoop, calls=%fused_computation.1295 | loop fusion | flops 35651584 | bytes 8392704 | tf_op jit(solution)/shard_map/convert.6
  575.1 10.2 %all-to-all-start.4 = ((bf16[64,2,256]{2,1,0:T(2,128)(2,1)}), bf16[64,2,256]{2,1,0:T(2,128)(2,1)S(1)}, u32[]{:S(2)}, u32[]{:S(2)}) async-start(bf16[64,2,256]{2,1,0:T(2,128)(2,1)} %reshape.4652), calls=%async_computation.4 | async-start | bytes 131072 | tf_op jit(solution)/shard_map/all_to_all | solution.py:162
  585.3 7.6 pad_maximum_fusion
  594.7 10.2 %all-to-all-start.6 = ((bf16[64,2,256]{2,1,0:T(2,128)(2,1)}), bf16[64,2,256]{2,1,0:T(2,128)(2,1)S(1)}, u32[]{:S(2)}, u32[]{:S(2)}) async-start(bf16[64,2,256]{2,1,0:T(2,128)(2,1)} %reshape.4656), calls=%async_computation.6 | async-start | bytes 131072 | tf_op jit(solution)/shard_map/all_to_all | solution.py:162
  611.1 7.6 all-to-all-start.8
  625.0 10.5 %all-to-all-start.10 = ((bf16[64,2,256]{2,1,0:T(2,128)(2,1)}), bf16[64,2,256]{2,1,0:T(2,128)(2,1)S(1)}, u32[]{:S(2)}, u32[]{:S(2)}) async-start(bf16[64,2,256]{2,1,0:T(2,128)(2,1)} %reshape.4664), calls=%async_computation.10 | async-start | bytes 131072 | tf_op jit(solution)/shard_map/all_to_all | solution.py:162
  641.9 8.3 fusion.526
  652.1 7.5 all-to-all-start.11
  659.6 8.3 fusion.520
  669.8 10.2 %all-to-all-start.9 = ((bf16[64,2,256]{2,1,0:T(2,128)(2,1)}), bf16[64,2,256]{2,1,0:T(2,128)(2,1)S(1)}, u32[]{:S(2)}, u32[]{:S(2)}) async-start(bf16[64,2,256]{2,1,0:T(2,128)(2,1)} %reshape.4662), calls=%async_computation.9 | async-start | bytes 131072 | tf_op jit(solution)/shard_map/all_to_all | solution.py:179
  679.9 8.3 fusion.514
  690.1 10.5 %all-to-all-start.7 = ((bf16[64,2,256]{2,1,0:T(2,128)(2,1)}), bf16[64,2,256]{2,1,0:T(2,128)(2,1)S(1)}, u32[]{:S(2)}, u32[]{:S(2)}) async-start(bf16[64,2,256]{2,1,0:T(2,128)(2,1)} %reshape.4658), calls=%async_computation.7 | async-start | bytes 131072 | tf_op jit(solution)/shard_map/all_to_all | solution.py:179
  700.6 8.3 fusion.508
  710.8 10.2 %all-to-all-start.5 = ((bf16[64,2,256]{2,1,0:T(2,128)(2,1)}), bf16[64,2,256]{2,1,0:T(2,128)(2,1)S(1)}, u32[]{:S(2)}, u32[]{:S(2)}) async-start(bf16[64,2,256]{2,1,0:T(2,128)(2,1)} %reshape.4654), calls=%async_computation.5 | async-start | bytes 131072 | tf_op jit(solution)/shard_map/all_to_all | solution.py:179
  721.0 8.3 fusion.502
  731.2 10.2 %all-to-all-start.3 = ((bf16[64,2,256]{2,1,0:T(2,128)(2,1)}), bf16[64,2,256]{2,1,0:T(2,128)(2,1)S(1)}, u32[]{:S(2)}, u32[]{:S(2)}) async-start(bf16[64,2,256]{2,1,0:T(2,128)(2,1)} %reshape.4650), calls=%async_computation.3 | async-start | bytes 131072 | tf_op jit(solution)/shard_map/all_to_all | solution.py:179
  741.4 8.3 fusion.496
  751.5 10.2 %all-to-all-start.1 = ((bf16[64,2,256]{2,1,0:T(2,128)(2,1)}), bf16[64,2,256]{2,1,0:T(2,128)(2,1)S(1)}, u32[]{:S(2)}, u32[]{:S(2)}) async-start(bf16[64,2,256]{2,1,0:T(2,128)(2,1)} %reshape.4646), calls=%async_computation.1 | async-start | bytes 131072 | tf_op jit(solution)/shard_map/all_to_all | solution.py:179
  762.9 5.1 all-to-all-done.1
  772.1 5.4 reshape.4621
  778.5 12.4 %fusion.461 = f32[16,512,6,2]{1,2,3,0:T(8,128)S(1)} fusion(bf16[512,16,512,1]{2,1,0,3:T(8,128)(2,1)} %bitcast.1493, bf16[6,16,2,512]{3,1,2,0:T(8,128)(2,1)S(1)} %get-tuple-element.1379), kind=kOutput, calls=%fused_computation.1305 | convolution fusion | flops 100663296 | bytes 8978432 | tf_op jit(solution)/shard_map/csmrj,imj->csmri/dot_general | solution.py:123
  790.8 12.5 %fusion.455 = f32[16,512,6,2]{1,2,3,0:T(8,128)S(1)} fusion(bf16[512,16,512,1]{2,1,0,3:T(8,128)(2,1)} %bitcast.1498, bf16[6,16,2,512]{3,1,2,0:T(8,128)(2,1)S(1)} %get-tuple-element.1380), kind=kOutput, calls=%fused_computation.1299 | convolution fusion | flops 100663296 | bytes 8978432 | tf_op jit(solution)/shard_map/csmrj,imj->csmri/dot_general | solution.py:126
  803.9 5.5 copy.300
  813.8 133.4 %all-reduce.2.cloned.1.call-done = bf16[6,16,2,1024]{1,3,2,0:T(8,128)(2,1)} async-done(((bf16[6,16,2,1024]{1,3,2,0:T(8,128)(2,1)}), bf16[6,16,2,1024]{1,3,2,0:T(8,128)(2,1)}) %all-reduce.2.cloned.1.call-update) | async-done | bytes 393232 | tf_op jit(solution)/shard_map/psum | solution.py:202
  (1082 shorter events, 177.8 us)
Async XLA Ops:
  8.4 453.0 %copy-start.2 = (bf16[6,1,16,2,1024]{4,3,2,1,0:T(2,128)(2,1)S(1)}, bf16[6,1,16,2,1024]{4,3,2,1,0:T(2,128)(2,1)}, u32[]{:S(2)}) copy-start(bf16[6,1,16,2,1024]{4,3,2,1,0:T(2,128)(2,1)} %param.6) | copy-start | bytes 1179652
  482.0 12.6 %slice-start = ((s8[8388608]{0:T(1024)(128)(4,1)}), s8[4194304]{0:T(1024)(128)(4,1)S(1)}, s32[]{:S(2)}) async-start(s8[8388608]{0:T(1024)(128)(4,1)} %bitcast.1494), calls=%async_computation.13 | async-start | bytes 8388608
  482.1 12.5 %slice-start.1 = ((s8[8388608]{0:T(1024)(128)(4,1)}), s8[4194304]{0:T(1024)(128)(4,1)S(1)}, s32[]{:S(2)}) async-start(s8[8388608]{0:T(1024)(128)(4,1)} %bitcast.1494), calls=%async_computation.14 | async-start | bytes 8388608
  503.8 18.5 %copy-start.3 = (s32[1024]{0:T(1024)S(1)}, s32[1024]{0:T(1024)}, u32[]{:S(2)}) copy-start(s32[1024]{0:T(1024)} %param.7) | copy-start | bytes 12292
  511.9 16.9 %all-to-all-start = ((bf16[64,2,256]{2,1,0:T(2,128)(2,1)}), bf16[64,2,256]{2,1,0:T(2,128)(2,1)S(1)}, u32[]{:S(2)}, u32[]{:S(2)}) async-start(bf16[64,2,256]{2,1,0:T(2,128)(2,1)} %reshape.4644), calls=%async_computation | async-start | bytes 131072 | tf_op jit(solution)/shard_map/all_to_all | solution.py:162
  528.8 46.3 %all-to-all-start.2 = ((bf16[64,2,256]{2,1,0:T(2,128)(2,1)}), bf16[64,2,256]{2,1,0:T(2,128)(2,1)S(1)}, u32[]{:S(2)}, u32[]{:S(2)}) async-start(bf16[64,2,256]{2,1,0:T(2,128)(2,1)} %reshape.4648), calls=%async_computation.2 | async-start | bytes 131072 | tf_op jit(solution)/shard_map/all_to_all | solution.py:162
  575.1 19.6 %all-to-all-start.4 = ((bf16[64,2,256]{2,1,0:T(2,128)(2,1)}), bf16[64,2,256]{2,1,0:T(2,128)(2,1)S(1)}, u32[]{:S(2)}, u32[]{:S(2)}) async-start(bf16[64,2,256]{2,1,0:T(2,128)(2,1)} %reshape.4652), calls=%async_computation.4 | async-start | bytes 131072 | tf_op jit(solution)/shard_map/all_to_all | solution.py:162
  585.3 56.6 %copy-start = (f32[1,16,2048]{2,1,0:T(8,128)S(1)}, f32[1,16,2048]{2,1,0:T(8,128)}, u32[]{:S(2)}) copy-start(f32[1,16,2048]{2,1,0:T(8,128)} %param.8) | copy-start | bytes 393220
  594.7 16.4 %all-to-all-start.6 = ((bf16[64,2,256]{2,1,0:T(2,128)(2,1)}), bf16[64,2,256]{2,1,0:T(2,128)(2,1)S(1)}, u32[]{:S(2)}, u32[]{:S(2)}) async-start(bf16[64,2,256]{2,1,0:T(2,128)(2,1)} %reshape.4656), calls=%async_computation.6 | async-start | bytes 131072 | tf_op jit(solution)/shard_map/all_to_all | solution.py:162
  611.1 13.9 %all-to-all-start.8 = ((bf16[64,2,256]{2,1,0:T(2,128)(2,1)}), bf16[64,2,256]{2,1,0:T(2,128)(2,1)S(1)}, u32[]{:S(2)}, u32[]{:S(2)}) async-start(bf16[64,2,256]{2,1,0:T(2,128)(2,1)} %reshape.4660), calls=%async_computation.8 | async-start | bytes 131072 | tf_op jit(solution)/shard_map/all_to_all | solution.py:162
  625.0 16.7 %all-to-all-start.10 = ((bf16[64,2,256]{2,1,0:T(2,128)(2,1)}), bf16[64,2,256]{2,1,0:T(2,128)(2,1)S(1)}, u32[]{:S(2)}, u32[]{:S(2)}) async-start(bf16[64,2,256]{2,1,0:T(2,128)(2,1)} %reshape.4664), calls=%async_computation.10 | async-start | bytes 131072 | tf_op jit(solution)/shard_map/all_to_all | solution.py:162
  652.1 17.6 %all-to-all-start.11 = ((bf16[64,2,256]{2,1,0:T(2,128)(2,1)}), bf16[64,2,256]{2,1,0:T(2,128)(2,1)S(1)}, u32[]{:S(2)}, u32[]{:S(2)}) async-start(bf16[64,2,256]{2,1,0:T(2,128)(2,1)} %reshape.4666), calls=%async_computation.11 | async-start | bytes 131072 | tf_op jit(solution)/shard_map/all_to_all | solution.py:179
  669.8 20.4 %all-to-all-start.9 = ((bf16[64,2,256]{2,1,0:T(2,128)(2,1)}), bf16[64,2,256]{2,1,0:T(2,128)(2,1)S(1)}, u32[]{:S(2)}, u32[]{:S(2)}) async-start(bf16[64,2,256]{2,1,0:T(2,128)(2,1)} %reshape.4662), calls=%async_computation.9 | async-start | bytes 131072 | tf_op jit(solution)/shard_map/all_to_all | solution.py:179
  690.1 20.7 %all-to-all-start.7 = ((bf16[64,2,256]{2,1,0:T(2,128)(2,1)}), bf16[64,2,256]{2,1,0:T(2,128)(2,1)S(1)}, u32[]{:S(2)}, u32[]{:S(2)}) async-start(bf16[64,2,256]{2,1,0:T(2,128)(2,1)} %reshape.4658), calls=%async_computation.7 | async-start | bytes 131072 | tf_op jit(solution)/shard_map/all_to_all | solution.py:179
  710.8 20.4 %all-to-all-start.5 = ((bf16[64,2,256]{2,1,0:T(2,128)(2,1)}), bf16[64,2,256]{2,1,0:T(2,128)(2,1)S(1)}, u32[]{:S(2)}, u32[]{:S(2)}) async-start(bf16[64,2,256]{2,1,0:T(2,128)(2,1)} %reshape.4654), calls=%async_computation.5 | async-start | bytes 131072 | tf_op jit(solution)/shard_map/all_to_all | solution.py:179
  731.2 20.4 %all-to-all-start.3 = ((bf16[64,2,256]{2,1,0:T(2,128)(2,1)}), bf16[64,2,256]{2,1,0:T(2,128)(2,1)S(1)}, u32[]{:S(2)}, u32[]{:S(2)}) async-start(bf16[64,2,256]{2,1,0:T(2,128)(2,1)} %reshape.4650), calls=%async_computation.3 | async-start | bytes 131072 | tf_op jit(solution)/shard_map/all_to_all | solution.py:179
  751.5 16.4 %all-to-all-start.1 = ((bf16[64,2,256]{2,1,0:T(2,128)(2,1)}), bf16[64,2,256]{2,1,0:T(2,128)(2,1)S(1)}, u32[]{:S(2)}, u32[]{:S(2)}) async-start(bf16[64,2,256]{2,1,0:T(2,128)(2,1)} %reshape.4646), calls=%async_computation.1 | async-start | bytes 131072 | tf_op jit(solution)/shard_map/all_to_all | solution.py:179
  761.7 185.4 %all-reduce.2.cloned.1.call-start = ((), (), s32[]{:S(2)}) async-start(), calls=%async_computation.12 | async-start | bytes 6291456 | tf_op jit(solution)/shard_map/psum | solution.py:202
  768.3 0.9 copy-start.1
Sparse Core Ops, SparseCore 0:
  809.5 137.5 all-reduce.1
where the time goes:
time: 975 us; the launch traced here: 957 us
  loops' own time  339 us (35%)
  waiting for transfers between devices  152 us (16%)
  other arithmetic  139 us (14%)
  starting transfers between devices  115 us (12%)
  local copies, waits for them, and re-layouts  100 us (10%)
  matrix products  96.4 us (10%)
  between operations  15.6 us (2%)
    another operation x1, loops' own time, legendre_tables(): lax.scan(pair_step, initial, jnp.arange(degree_count // 2, dtype=jnp.int3...  339 us
    psum x1, waiting for transfers between devices, shards(): lax.psum(weighted.astype(jnp.bfloat16), 'shell').astype(jnp.float32)  133 us
    all_to_all x6, starting transfers between devices, shards(): lax.all_to_all(spectra.reshape(cycle_item_count, shell_count, block_count...  58.7 us
    while x496, other arithmetic  56.9 us
    all_to_all x6, starting transfers between devices, shards(): lax.all_to_all(outgoing[component:component + 1], 'blk', split_axis=2, co...  56.2 us
    dot_general x6, matrix products, shards(): jnp.einsum('csjk,dxrk->csdxrj', stress, wave_table, preferred_element_typ...  49.8 us
    another operation x4, other arithmetic  37.2 us
    slice x32, local copies, waits for them, and re-layouts, legendre_tables(): lax.scan(pair_step, initial, jnp.arange(degree_count // 2, dtype=jnp.int3...  23.3 us
  transfers between devices with their start and end apart: 13, of which 5 were waited for; matrix products, arithmetic and copies ran while one was open for 12% of the time, Pallas kernels for 0%

commit v1 on v0

v1 whole, which is shorter than its diff:
```python
import functools
import math

import jax
import jax.numpy as jnp
import numpy as np
from jax import lax
from jax.experimental import pallas as pl
from jax.experimental.pallas import tpu as pltpu
from jax.sharding import PartitionSpec as P

F32 = jnp.float32
BF16 = jnp.bfloat16
COMPS = 6
PARTS = 2
ORDERS = 16
DEG = 1024
HALF = 512
BLK = 64
CYC = 16
POINTS = 2048
KH = POINTS // 2
LB = 256
LSTRIDE = LB + 1
TILES = HALF // 128
BIG = 2.0**40
SMALL = 2.0**-40
NT = (((1,), (1,)), ((), ()))


def latitude_constants():
    j = np.arange(HALF, dtype=np.float64)
    theta = np.pi * (2.0 * j + 1.0) / (4.0 * HALF)
    x = np.cos(theta)
    logsin = np.log2(np.sin(theta))
    hi = np.round(logsin * 512.0) / 512.0
    lo = logsin - hi
    k = np.arange(1, HALF + 1, dtype=np.float64)
    phase = np.outer(k, 2.0 * j + 1.0) % (4.0 * HALF)
    series = np.sum(np.cos(phase * np.pi / (2.0 * HALF)) / (4.0 * k * k - 1.0)[:, None], axis=0)
    weight = (2.0 / (2.0 * HALF)) * (1.0 - 2.0 * series)
    m = np.arange(DEG, dtype=np.float64)
    fac = np.concatenate([[0.0], np.cumsum(np.log2(1.0 - 0.5 / np.arange(1, DEG)))])
    g = 0.5 * np.log2((2.0 * m + 1.0) / (4.0 * np.pi)) + 0.5 * fac
    lat = np.stack([x, hi, lo, weight]).astype(np.float32)
    return np.concatenate([lat, np.zeros((4, HALF), np.float32)]), g.astype(np.float32)[None]


def legendre_kernel(ord_ref, mb_ref, lat_ref, g_ref, spec_ref, tab_ref, msg_ref, ca, cab, prev, cur, ini, expo, ft, acc, lhs, ns):
    step = pl.program_id(0)

    @pl.when(step == 0)
    def _():
        lane = lax.broadcasted_iota(jnp.int32, (8, 128), 1).astype(F32)
        glane = lax.broadcasted_iota(jnp.int32, (8, DEG), 1).astype(F32)
        for par in range(2):
            m = mb_ref[par]
            for b in range(DEG // 128):
                l = lane + float(128 * b)
                up = l > m
                den = jnp.where(up, (l - m) * (l + m), 1.0)
                a2 = (4.0 * l * l - 1.0) / den
                a = jnp.where(up, jnp.sqrt(jnp.where(up, a2, 1.0)), 0.0)
                below = l - 1.0
                top = jnp.where(below > m, (below - m) * (below + m), 0.0)
                b2 = top / jnp.maximum(4.0 * below * below - 1.0, 1.0)
                ca[b, par] = a
                cab[b, par] = a * jnp.sqrt(b2)
            gm = jnp.sum(jnp.where(glane == m[:, :1], g_ref[...], 0.0), axis=1, keepdims=True)
            for t in range(TILES):
                cols = pl.ds(128 * t, 128)
                mh = m * lat_ref[1:2, cols]
                whole = jnp.floor(mh)
                frac = (mh - whole) + m * lat_ref[2:3, cols] + gm
                ini[par, t] = jnp.exp(frac * math.log(2.0))
                expo[par, t] = whole
                prev[par, t] = jnp.zeros((8, 128), F32)
                cur[par, t] = jnp.zeros((8, 128), F32)

        deg = lax.broadcasted_iota(jnp.int32, (16, DEG), 1)

        def place(q, _):
            par, p = q // 8, q % 8
            slot = 2 * p + ((ord_ref[2 * p] + par) & 1)
            order = ord_ref[slot]
            rows = [spec_ref[c, slot].astype(F32) for c in range(COMPS)]
            rows.append(jnp.zeros((4, DEG), F32))
            data = jnp.concatenate(rows, axis=0) * jnp.where(order == 0, 1.0, 2.0)
            even = ((deg + order) & 1) == 0
            lhs[q, 0:16] = jnp.where(even, data, 0.0).astype(BF16)
            lhs[q, 16:32] = jnp.where(even, 0.0, data).astype(BF16)
            acc[q] = jnp.zeros((32, HALF), F32)
            return 0

        lax.fori_loop(0, ORDERS, place, 0)

    def eight(sub, _):
        block = step * (LB // 128) + sub // 16
        shift = (128 - 8 * (sub % 16)) % 128
        base = step * LB + sub * 8
        av = [pltpu.roll(ca[block, par], shift, 1) for par in range(2)]
        abv = [pltpu.roll(cab[block, par], shift, 1) for par in range(2)]
        xs = [jnp.broadcast_to(lat_ref[0:1, pl.ds(128 * t, 128)], (8, 128)) for t in range(TILES)]
        for par in range(2):
            m = mb_ref[par]
            state = []
            for t in range(TILES):
                e = expo[par, t]
                c, p = cur[par, t], prev[par, t]
                big = jnp.abs(c) > BIG
                f = jnp.where(big, SMALL, 1.0)
                e = jnp.where(big, e + 40.0, e)
                expo[par, t] = e
                scale = jnp.where(e < -126.0, 0.0, jnp.exp(jnp.maximum(e, -126.0) * math.log(2.0)))
                state.append((p * f, c * f, scale, ini[par, t]))
            for r in range(8):
                a = jnp.broadcast_to(av[par][:, r : r + 1], (8, 128))
                ab = jnp.broadcast_to(abv[par][:, r : r + 1], (8, 128))
                hit = m == (base + r).astype(F32)
                for t in range(TILES):
                    p, c, scale, start = state[t]
                    new = (a * xs[t]) * c - ab * p
                    new = jnp.where(hit, start, new)
                    state[t] = (c, new, scale, start)
                    ft[t, pl.ds(par * 8 * LSTRIDE + sub * 8 + r, 8, stride=LSTRIDE), :] = new * scale
            for t in range(TILES):
                prev[par, t] = state[t][0]
                cur[par, t] = state[t][1]
        return 0

    lax.fori_loop(0, LB // 8, eight, 0)

    for q in range(ORDERS):
        table = jnp.concatenate([ft[t, q * LSTRIDE : q * LSTRIDE + LB, :] for t in range(TILES)], axis=1).astype(BF16)
        tab_ref[q] = table
        left = lhs[q, :, pl.ds(pl.multiple_of(step * LB, LB), LB)]
        acc[q] += jnp.dot(left, table, preferred_element_type=F32)

    @pl.when(step == pl.num_programs(0) - 1)
    def _():
        def spread(q, _):
            sym, anti = acc[q, 0:16], acc[q, 16:32]
            for t in range(TILES):
                cols = slice(128 * t, 128 * t + 128)
                ns[t, pl.ds(q, 16, stride=16), :] = sym[:, cols] + anti[:, cols]
                ns[TILES + t, pl.ds(q, 16, stride=16), :] = sym[:, cols] - anti[:, cols]
            return 0

        lax.fori_loop(0, ORDERS, spread, 0)
        for t in range(2 * TILES):
            flipped = jnp.concatenate([ns[t, 0:128].T, ns[t, 128:256].T], axis=1).astype(BF16)
            for b in range(8):
                d = (t % TILES) * 8 + b
                dest = d if t < TILES else BLK - 1 - d
                msg_ref[dest] = flipped[16 * b : 16 * b + 16]


def run_legendre(my_orders, mb, lat, g, spec):
    full = lambda shape: pl.BlockSpec(shape, lambda i: (0,) * len(shape))
    return pl.pallas_call(
        legendre_kernel,
        grid=(DEG // LB,),
        in_specs=[
            pl.BlockSpec(memory_space=pltpu.SMEM),
            full((2, 8, 128)),
            full((8, HALF)),
            full((1, DEG)),
            full((COMPS, ORDERS, PARTS, DEG)),
        ],
        out_specs=[
            pl.BlockSpec((ORDERS, LB, HALF), lambda i: (0, i, 0)),
            full((BLK, CYC, 256)),
        ],
        out_shape=[
            jax.ShapeDtypeStruct((ORDERS, DEG, HALF), BF16),
            jax.ShapeDtypeStruct((BLK, CYC, 256), BF16),
        ],
        scratch_shapes=[
            pltpu.VMEM((DEG // 128, 2, 8, 128), F32),
            pltpu.VMEM((DEG // 128, 2, 8, 128), F32),
            pltpu.VMEM((2, TILES, 8, 128), F32),
            pltpu.VMEM((2, TILES, 8, 128), F32),
            pltpu.VMEM((2, TILES, 8, 128), F32),
            pltpu.VMEM((2, TILES, 8, 128), F32),
            pltpu.VMEM((TILES, ORDERS * LSTRIDE + 8, 128), F32),
            pltpu.VMEM((ORDERS, 32, HALF), F32),
            pltpu.VMEM((ORDERS, 32, DEG), BF16),
            pltpu.VMEM((2 * TILES, 256, 128), F32),
        ],
        name="legendre",
    )(my_orders, mb, lat, g, spec)


def turn(phase):
    t = phase * (1.0 / KH) - 1.0
    z = t * t
    c = jnp.full_like(z, 0.0)
    s = jnp.full_like(z, 0.0)
    for i in range(8, -1, -1):
        c = c * z + float((-1) ** (i + 1) * math.pi ** (2 * i) / math.factorial(2 * i))
        s = s * z + float((-1) ** (i + 1) * math.pi ** (2 * i + 1) / math.factorial(2 * i + 1))
    return c, s * t


def wrap(value):
    return value - POINTS * jnp.floor(value * (1.0 / POINTS))


def longitude_kernel(flip_ref, me_ref, shift_ref, vis_ref, msg_ref, out_ref, wave, left, pm, spect, vis):
    lane = lax.broadcasted_iota(jnp.int32, (8, 128), 1).astype(F32)
    sc, ss = [], []
    for u in range(KH // 128):
        sc.append(jnp.broadcast_to(shift_ref[0:1, pl.ds(128 * u, 128)], (8, 128)))
        ss.append(jnp.broadcast_to(shift_ref[1:2, pl.ds(128 * u, 128)], (8, 128)))

    def make(src, _):
        m = me_ref[src]
        c, s = turn(wrap(m * lane))
        gc, gs = turn(wrap(m * 128.0))
        for u in range(KH // 128):
            oc = sc[u] * c - ss[u] * s
            os = -(ss[u] * c + sc[u] * s)
            rows = pl.ds(pl.multiple_of(src * 32, 32), 32)
            wave[rows, pl.ds(128 * u, 128)] = jnp.concatenate([c, oc, -s, -os], axis=0).astype(BF16)
            c, s = c * gc - s * gs, s * gc + c * gs
        return 0

    lax.fori_loop(0, BLK, make, 0)

    flip = flip_ref[0]
    for j in range(CYC):
        row = jnp.where(flip == 1, CYC - 1 - j, j)
        vis[j : j + 1, :] = vis_ref[pl.ds(row, 1), :]

    wide = lax.broadcasted_iota(jnp.int32, (16, 128), 1)
    even = ((wide // 8) % 2) == 0
    quarter = wide // 32
    for g in range(BLK // 4):
        pieces = [[msg_ref[4 * g + i, :, pl.ds(128 * h, 128)].astype(F32) for h in range(2)] for i in range(4)]
        for c in range(COMPS):
            total = None
            for i in range(4):
                piece = pieces[i][c // 4]
                shift = (32 * (i - c)) % 128
                moved = pltpu.roll(piece, shift, 1) if shift else piece
                total = moved if total is None else jnp.where(quarter == i, moved, total)
            left[16 * c : 16 * c + 16, pl.ds(128 * g, 128)] = jnp.where(even, total, 0.0).astype(BF16)
            left[96 + 16 * c : 112 + 16 * c, pl.ds(128 * g, 128)] = jnp.where(even, 0.0, total).astype(BF16)

    for u in range(KH // 256):
        cols = pl.ds(256 * u, 256)
        field = jnp.dot(left[...], wave[:, cols], preferred_element_type=F32)
        low, high = vis[:, cols], vis[:, pl.ds(KH + 256 * u, 256)]
        for c in range(COMPS):
            e, o = field[16 * c : 16 * c + 16], field[96 + 16 * c : 112 + 16 * c]
            first, second = low * (e + o), high * (e - o)
            pm[16 * c : 16 * c + 16, cols] = (first + second).astype(BF16)
            pm[96 + 16 * c : 112 + 16 * c, cols] = (first - second).astype(BF16)

    def back(b, _):
        rows = pl.ds(pl.multiple_of(b * 256, 256), 256)
        both = lax.dot_general(pm[...], wave[rows, :], NT, preferred_element_type=F32)
        lanes = lax.broadcasted_iota(jnp.int32, (96, 256), 1)
        pick = ((lanes // 8) % 2) == 0
        spect[:, rows] = jnp.where(pick, both[:96], both[96:]) * (2.0 * math.pi / POINTS)
        return 0

    lax.fori_loop(0, POINTS // 256, back, 0)

    for g in range(BLK // 4):
        vals = [spect[16 * c : 16 * c + 16, pl.ds(128 * g, 128)] for c in range(COMPS)]
        for i in range(4):
            for h in range(2):
                total = None
                for c in range(4 * h, min(4 * h + 4, COMPS)):
                    shift = (32 * (c - i)) % 128
                    moved = pltpu.roll(vals[c], shift, 1) if shift else vals[c]
                    total = moved if total is None else jnp.where(quarter == c % 4, moved, total)
                out_ref[4 * g + i, :, pl.ds(128 * h, 128)] = total.astype(BF16)


def run_longitude(flip, me, shift, vis, msg):
    whole = pl.BlockSpec(memory_space=pltpu.VMEM)
    return pl.pallas_call(
        longitude_kernel,
        in_specs=[pl.BlockSpec(memory_space=pltpu.SMEM), whole, whole, whole, whole],
        out_specs=whole,
        out_shape=jax.ShapeDtypeStruct((BLK, CYC, 256), BF16),
        scratch_shapes=[
            pltpu.VMEM((POINTS, KH), BF16),
            pltpu.VMEM((192, POINTS), BF16),
            pltpu.VMEM((192, KH), BF16),
            pltpu.VMEM((96, POINTS), F32),
            pltpu.VMEM((CYC, POINTS), F32),
        ],
        name="longitude",
    )(flip, me, shift, vis, msg)


def analysis_kernel(ord_ref, rad_ref, lat_ref, tab_ref, msg_ref, out_ref, sum_ref, side):
    q = pl.program_id(0)

    @pl.when(q == 0)
    def _():
        for t in range(TILES):
            w = lat_ref[3:4, pl.ds(128 * t, 128)]
            for h in range(2):
                lanes = pl.ds(128 * h, 128)
                north = jnp.concatenate([msg_ref[8 * t + b, :, lanes].astype(F32) for b in range(8)], axis=0)
                south = jnp.concatenate([msg_ref[BLK - 1 - 8 * t - b, :, lanes].astype(F32) for b in range(8)], axis=0)
                side[t, 0, pl.ds(128 * h, 128), :] = (north + south).T * w
                side[t, 1, pl.ds(128 * h, 128), :] = (north - south).T * w

    par, p = q // 8, q % 8
    slot = 2 * p + ((ord_ref[2 * p] + par) & 1)
    order = ord_ref[slot]
    left = jnp.concatenate(
        [
            jnp.concatenate([side[t, half, pl.ds(q, 16, stride=16), :] for t in range(TILES)], axis=1)
            for half in range(2)
        ],
        axis=0,
    ).astype(BF16)
    both = lax.dot_general(left, tab_ref[0], NT, preferred_element_type=F32)
    deg = lax.broadcasted_iota(jnp.int32, (16, DEG), 1)
    coef = jnp.where(((deg + order) & 1) == 0, both[:16], both[16:])
    scaled = coef * rad_ref[0]
    for c in range(COMPS):
        out_ref[c, slot] = coef[2 * c : 2 * c + 2].astype(BF16)
        sum_ref[c, slot] = scaled[2 * c : 2 * c + 2].astype(BF16)


def run_analysis(my_orders, rad, lat, tab, msg):
    full = lambda shape: pl.BlockSpec(shape, lambda i: (0,) * len(shape))
    shape = (COMPS, ORDERS, PARTS, DEG)
    return pl.pallas_call(
        analysis_kernel,
        grid=(ORDERS,),
        in_specs=[
            pl.BlockSpec(memory_space=pltpu.SMEM),
            pl.BlockSpec(memory_space=pltpu.SMEM),
            full((8, HALF)),
            pl.BlockSpec((1, DEG, HALF), lambda i: (i, 0, 0)),
            full((BLK, CYC, 256)),
        ],
        out_specs=[full(shape), full(shape)],
        out_shape=[jax.ShapeDtypeStruct(shape, BF16)] * 2,
        scratch_shapes=[pltpu.VMEM((TILES, 2, 256, 128), F32)],
        name="analysis",
    )(my_orders, rad, lat, tab, msg)


def order_columns(order_map, index):
    pairs = order_map.reshape(-1, 2)
    evens = jnp.where(pairs[:, 0] % 2 == 0, pairs[:, 0], pairs[:, 1]).astype(F32)
    me = jnp.broadcast_to(evens.reshape(BLK, 8, 1), (BLK, 8, 128))
    mine = lax.dynamic_slice_in_dim(evens, index * 8, 8)
    mb = jnp.broadcast_to(jnp.stack([mine, (DEG - 1.0) - mine])[:, :, None], (2, 8, 128))
    return me, mb


def shift_table():
    k = np.arange(KH, dtype=np.float64)
    ang = 2.0 * np.pi * k / POINTS
    sign = 1.0 - 2.0 * (k % 2)
    return np.stack([sign * np.cos(ang), sign * np.sin(ang)]).astype(np.float32)


def shards(strain_spec, order_map, viscosity, radial_weight):
    index = lax.axis_index("blk")
    lat, g = latitude_constants()
    lat, g = jnp.asarray(lat), jnp.asarray(g)
    my_orders = lax.dynamic_slice_in_dim(order_map, index * ORDERS, ORDERS)
    me, mb = order_columns(order_map, index)
    tab, msg = run_legendre(my_orders, mb, lat, g, strain_spec.reshape(COMPS, ORDERS, PARTS, DEG))
    msg = lax.all_to_all(msg, "blk", split_axis=0, concat_axis=0, tiled=True)
    flip = (index >= BLK // 2).astype(jnp.int32).reshape(1)
    msg = run_longitude(flip, me, jnp.asarray(shift_table()), viscosity.reshape(CYC, POINTS), msg)
    msg = lax.all_to_all(msg, "blk", split_axis=0, concat_axis=0, tiled=True)
    spec, part = run_analysis(my_orders, radial_weight, lat, tab, msg)
    summed = lax.psum_scatter(part, "shell", scatter_dimension=3, tiled=True)
    return spec.reshape(strain_spec.shape), summed.astype(F32)


def solution(mesh):
    return jax.shard_map(
        shards,
        mesh=mesh,
        in_specs=(P(None, "shell", "blk", None, None), P(), P("shell", "blk", None), P("shell")),
        out_specs=(P(None, "shell", "blk", None, None), P(None, "blk", None, "shell")),
        check_vma=False,
    )
```

time: 975 us -> 270 us (0.28)
  the two profiles are of different devices: /device:TPU:97 before, /device:TPU:1 now
where the time goes in v1:
time: 270 us; the launch traced here: 269 us
  local copies, waits for them, and re-layouts  104 us (39%)
  waiting for transfers between devices  70 us (26%)
  Pallas kernels  61.2 us (23%)
  starting transfers between devices  18 us (7%)
  between operations  14.7 us (5%)
    unnamed x8, local copies, waits for them, and re-layouts  99.8 us
    unnamed x2, waiting for transfers between devices  38.3 us
    pallas_call x1, Pallas kernels, run_legendre(): pl.pallas_call(legendre_kernel, grid=(DEG // LB,), in_specs=[pl.BlockSpec...  35.5 us
    all_to_all x2, waiting for transfers between devices, shards(): msg = lax.all_to_all(msg, 'blk', split_axis=0, concat_axis=0, tiled=True)  31.8 us
    all_to_all x2, starting transfers between devices, shards(): msg = lax.all_to_all(msg, 'blk', split_axis=0, concat_axis=0, tiled=True)  17.8 us
    pallas_call x1, Pallas kernels, run_analysis(): pl.pallas_call(analysis_kernel, grid=(ORDERS,), in_specs=[pl.BlockSpec(me...  15.8 us
    pallas_call x1, Pallas kernels, run_longitude(): pl.pallas_call(longitude_kernel, in_specs=[pl.BlockSpec(memory_space=pltp...  9.78 us
  transfers between devices with their start and end apart: 3, of which 3 were waited for; matrix products, arithmetic and copies ran while one was open for 0% of the time, Pallas kernels for 0%

profile of v1, /device:TPU:1, one launch (start us, length us, event | category | flops | bytes accessed | tf_op | source)
XLA Modules:
  0.0 268.8 jit_solution(14429020069105866720)
XLA Ops:
  7.2 0.9 reshape.54
  8.1 1.3 dynamic_slice.6.ord_ref
  9.3 0.3 slice_reduce_fusion
  9.6 0.1 dynamic-slice_bitcast_fusion
  9.7 0.7 broadcast_in_dim.4.mb_ref
  10.4 35.5 %legendre.1 = (bf16[16,1024,512]{2,1,0:T(8,128)(2,1)}, bf16[64,16,256]{2,1,0:T(8,128)(2,1)}) custom-call(s32[16]{0:T(128)} %dynamic_slice.6.ord_ref, f32[2,8,128]{2,1,0:T(8,128)} %broadcast_in_dim.4.mb_ref, f32[8,512]{1,0:T(8,128)} %constant.41.clone.lat_ref, f32[1,1024]{1,0:T(1,128)} %constant.42.clone.g_ref, bf16[6,16,2,1024]{3,2,1,0:T(2,128)(2,1)} %bitcast.16), custom_call_target="tpu_custom_call" | custom-call | tf_op jit(solution)/shard_map/legendre/pallas_call | solution.py:160
  46.0 12.5 %all-to-all-start = ((bf16[64,16,256]{2,1,0:T(8,128)(2,1)}), bf16[64,16,256]{2,1,0:T(8,128)(2,1)S(1)}, u32[]{:S(2)}, u32[]{:S(2)}) async-start(bf16[64,16,256]{2,1,0:T(8,128)(2,1)} %get-tuple-element.7), calls=%async_computation | async-start | bytes 1048576 | tf_op jit(solution)/shard_map/all_to_all | solution.py:376
  58.5 0.1 squeeze.14
  58.6 0.1 squeeze.13
  58.7 16.7 %all-to-all-done.msg_ref = bf16[64,16,256]{2,1,0:T(8,128)(2,1)S(1)} async-done(((bf16[64,16,256]{2,1,0:T(8,128)(2,1)}), bf16[64,16,256]{2,1,0:T(8,128)(2,1)S(1)}, u32[]{:S(2)}, u32[]{:S(2)}) %all-to-all-start) | async-done | bytes 524320 | tf_op jit(solution)/shard_map/all_to_all | solution.py:376
  75.5 0.0 copy-start.1
  75.5 0.9 broadcast_in_dim.5.me_ref
  76.3 0.0 copy-done.1
  76.3 9.8 %longitude.1 = bf16[64,16,256]{2,1,0:T(8,128)(2,1)} custom-call(s32[1]{0:T(128)} %bitcast.5.flip_ref, f32[64,8,128]{2,1,0:T(8,128)} %broadcast_in_dim.5.me_ref, f32[2,1024]{1,0:T(2,128)} %constant.43.clone.shift_ref, f32[16,2048]{1,0:T(8,128)} %bitcast.17, bf16[64,16,256]{2,1,0:T(8,128)(2,1)} %copy-done.1), custom_call_target="tpu_custom_call" | custom-call | tf_op jit(solution)/shard_map/longitude/pallas_call | solution.py:284
  86.1 5.2 %all-to-all-start.1 = ((bf16[64,16,256]{2,1,0:T(8,128)(2,1)}), bf16[64,16,256]{2,1,0:T(8,128)(2,1)S(1)}, u32[]{:S(2)}, u32[]{:S(2)}) async-start(bf16[64,16,256]{2,1,0:T(8,128)(2,1)} %longitude.1), calls=%async_computation.1 | async-start | bytes 1048576 | tf_op jit(solution)/shard_map/all_to_all | solution.py:379
  91.4 0.2 reduce-scatter.4.cloned.1.call-start
  92.2 15.0 %all-to-all-done.1.msg_ref = bf16[64,16,256]{2,1,0:T(8,128)(2,1)S(1)} async-done(((bf16[64,16,256]{2,1,0:T(8,128)(2,1)}), bf16[64,16,256]{2,1,0:T(8,128)(2,1)S(1)}, u32[]{:S(2)}, u32[]{:S(2)}) %all-to-all-start.1) | async-done | bytes 524320 | tf_op jit(solution)/shard_map/all_to_all | solution.py:379
  107.3 0.0 copy-start
  107.3 0.8 copy-done
  108.1 15.8 %analysis.1 = (bf16[6,16,2,1024]{3,2,1,0:T(2,128)(2,1)}, bf16[6,16,2,1024]{3,2,1,0:T(2,128)(2,1)}) custom-call(s32[16]{0:T(128)} %dynamic_slice.6.ord_ref, f32[1]{0:T(128)S(6)} %copy.15.rad_ref, f32[8,512]{1,0:T(8,128)} %constant.41.clone.lat_ref, bf16[16,1024,512]{2,1,0:T(8,128)(2,1)} %get-tuple-element.6.tab_ref, bf16[64,16,256]{2,1,0:T(8,128)(2,1)} %copy-done), custom_call_target="tpu_custom_call" | custom-call | tf_op jit(solution)/shard_map/analysis/pallas_call | solution.py:336
  123.9 39.6 %copy.13 = bf16[6,16,2,1024]{2,1,0,3:T(8,128)(2,1)} copy(bf16[6,16,2,1024]{3,2,1,0:T(2,128)(2,1)} %get-tuple-element.9) | data formatting | bytes 786432
  163.5 36.5 %reshape.62 = bf16[1024,192]{1,0:T(8,128)(2,1)} reshape(bf16[1024,6,16,2]{3,2,1,0:T(8,128)(2,1)} %bitcast.14) | data formatting | bytes 786432
  200.1 0.0 reduce-scatter.4.cloned.1.call-update
  200.1 38.3 %reduce-scatter.4.cloned.1.call-done = bf16[256,192]{1,0:T(8,128)(2,1)} async-done(((bf16[1024,192]{1,0:T(8,128)(2,1)}), bf16[256,192]{1,0:T(8,128)(2,1)}) %reduce-scatter.4.cloned.1.call-update) | async-done | bytes 98320
  238.4 14.9 %reshape.63 = bf16[256,6,16,2]{3,2,1,0:T(8,128)(2,1)} reshape(bf16[256,192]{1,0:T(8,128)(2,1)} %reduce-scatter.4.cloned.1.call-done) | data formatting | bytes 196608
  253.2 8.0 %copy.14 = bf16[6,16,2,256]{3,2,1,0:T(2,128)(2,1)S(1)} copy(bf16[6,16,2,256]{2,1,0,3:T(8,128)(2,1)} %bitcast.15) | data formatting | bytes 196608
  261.2 0.7 convert_element_type.15
  (3 shorter events, 0.0 us)
Async XLA Ops:
  46.0 29.5 %all-to-all-start = ((bf16[64,16,256]{2,1,0:T(8,128)(2,1)}), bf16[64,16,256]{2,1,0:T(8,128)(2,1)S(1)}, u32[]{:S(2)}, u32[]{:S(2)}) async-start(bf16[64,16,256]{2,1,0:T(8,128)(2,1)} %get-tuple-element.7), calls=%async_computation | async-start | bytes 1048576 | tf_op jit(solution)/shard_map/all_to_all | solution.py:376
  75.5 0.9 copy-start.1
  86.1 21.1 %all-to-all-start.1 = ((bf16[64,16,256]{2,1,0:T(8,128)(2,1)}), bf16[64,16,256]{2,1,0:T(8,128)(2,1)S(1)}, u32[]{:S(2)}, u32[]{:S(2)}) async-start(bf16[64,16,256]{2,1,0:T(8,128)(2,1)} %longitude.1), calls=%async_computation.1 | async-start | bytes 1048576 | tf_op jit(solution)/shard_map/all_to_all | solution.py:379
  91.4 147.0 %reduce-scatter.4.cloned.1.call-start = ((), (), s32[]{:S(2)}) async-start(), calls=%async_computation.3 | async-start | bytes 655360
  107.3 0.8 copy-start
Sparse Core Ops, SparseCore 0:
  200.2 38.1 reduce-scatter.3

commit v2 on v1

--- a/solution.py
+++ b/solution.py
@@ -17,6 +17,7 @@
 DEG = 1024
 HALF = 512
 BLK = 64
+SHELLS = 4
 CYC = 16
 POINTS = 2048
 KH = POINTS // 2
@@ -26,6 +27,7 @@
 BIG = 2.0**40
 SMALL = 2.0**-40
 NT = (((1,), (1,)), ((), ()))
+MESH = pl.DeviceIdType.MESH
 
 
 def latitude_constants():
@@ -206,7 +208,31 @@
     return value - POINTS * jnp.floor(value * (1.0 / POINTS))
 
 
-def longitude_kernel(flip_ref, me_ref, shift_ref, vis_ref, msg_ref, out_ref, wave, left, pm, spect, vis):
+def longitude_kernel(me_ref, shift_ref, vis_ref, msg_ref, out_ref, wave, left, pm, spect, vis, got, give, sems):
+    here = lax.axis_index("blk")
+    barrier = pltpu.get_barrier_semaphore()
+
+    def greet(i, _):
+        pl.semaphore_signal(barrier, inc=1, device_id={"blk": lax.rem(here + i, BLK)}, device_id_type=MESH)
+        return 0
+
+    lax.fori_loop(1, BLK, greet, 0)
+    pl.semaphore_wait(barrier, BLK - 1)
+
+    def first_copy(peer, mine):
+        return pltpu.make_async_remote_copy(
+            src_ref=msg_ref.at[peer], dst_ref=got.at[mine], send_sem=sems.at[0], recv_sem=sems.at[1],
+            device_id={"blk": peer}, device_id_type=MESH,
+        )
+
+    def send_first(i, _):
+        first_copy(lax.rem(here + i, BLK), here).start()
+        return 0
+
+    lax.fori_loop(1, BLK, send_first, 0)
+    own = pltpu.make_async_copy(msg_ref.at[here], got.at[here], sems.at[4])
+    own.start()
+
     lane = lax.broadcasted_iota(jnp.int32, (8, 128), 1).astype(F32)
     sc, ss = [], []
     for u in range(KH // 128):
@@ -227,16 +253,21 @@
 
     lax.fori_loop(0, BLK, make, 0)
 
-    flip = flip_ref[0]
     for j in range(CYC):
-        row = jnp.where(flip == 1, CYC - 1 - j, j)
+        row = jnp.where(here >= BLK // 2, CYC - 1 - j, j)
         vis[j : j + 1, :] = vis_ref[pl.ds(row, 1), :]
+
+    own.wait()
+    pltpu.make_async_remote_copy(
+        src_ref=msg_ref.at[0 : BLK - 1], dst_ref=got.at[0 : BLK - 1], send_sem=sems.at[0], recv_sem=sems.at[1],
+        device_id={"blk": here}, device_id_type=MESH,
+    ).wait()
 
     wide = lax.broadcasted_iota(jnp.int32, (16, 128), 1)
     even = ((wide // 8) % 2) == 0
     quarter = wide // 32
     for g in range(BLK // 4):
-        pieces = [[msg_ref[4 * g + i, :, pl.ds(128 * h, 128)].astype(F32) for h in range(2)] for i in range(4)]
+        pieces = [[got[4 * g + i, :, pl.ds(128 * h, 128)].astype(F32) for h in range(2)] for i in range(4)]
         for c in range(COMPS):
             total = None
             for i in range(4):
@@ -267,8 +298,9 @@
 
     lax.fori_loop(0, POINTS // 256, back, 0)
 
-    for g in range(BLK // 4):
-        vals = [spect[16 * c : 16 * c + 16, pl.ds(128 * g, 128)] for c in range(COMPS)]
+    def pack(g, _):
+        cols = pl.ds(pl.multiple_of(g * 128, 128), 128)
+        vals = [spect[16 * c : 16 * c + 16, cols] for c in range(COMPS)]
         for i in range(4):
             for h in range(2):
                 total = None
@@ -276,15 +308,35 @@
                     shift = (32 * (c - i)) % 128
                     moved = pltpu.roll(vals[c], shift, 1) if shift else vals[c]
                     total = moved if total is None else jnp.where(quarter == c % 4, moved, total)
-                out_ref[4 * g + i, :, pl.ds(128 * h, 128)] = total.astype(BF16)
-
-
-def run_longitude(flip, me, shift, vis, msg):
+                give[4 * g + i, :, pl.ds(128 * h, 128)] = total.astype(BF16)
+        return 0
+
+    lax.fori_loop(0, BLK // 4, pack, 0)
+
+    def send_second(i, _):
+        peer = lax.rem(here + i, BLK)
+        pltpu.make_async_remote_copy(
+            src_ref=give.at[peer], dst_ref=out_ref.at[here], send_sem=sems.at[2], recv_sem=sems.at[3],
+            device_id={"blk": peer}, device_id_type=MESH,
+        ).start()
+        return 0
+
+    lax.fori_loop(1, BLK, send_second, 0)
+    own = pltpu.make_async_copy(give.at[here], out_ref.at[here], sems.at[4])
+    own.start()
+    own.wait()
+    pltpu.make_async_remote_copy(
+        src_ref=give.at[0 : BLK - 1], dst_ref=out_ref.at[0 : BLK - 1], send_sem=sems.at[2], recv_sem=sems.at[3],
+        device_id={"blk": here}, device_id_type=MESH,
+    ).wait()
+
+
+def run_longitude(me, shift, vis, msg):
     whole = pl.BlockSpec(memory_space=pltpu.VMEM)
     return pl.pallas_call(
         longitude_kernel,
-        in_specs=[pl.BlockSpec(memory_space=pltpu.SMEM), whole, whole, whole, whole],
-        out_specs=whole,
+        in_specs=[whole] * 4,
+        out_specs=pl.BlockSpec(memory_space=pl.ANY),
         out_shape=jax.ShapeDtypeStruct((BLK, CYC, 256), BF16),
         scratch_shapes=[
             pltpu.VMEM((POINTS, KH), BF16),
@@ -292,9 +344,51 @@
             pltpu.VMEM((192, KH), BF16),
             pltpu.VMEM((96, POINTS), F32),
             pltpu.VMEM((CYC, POINTS), F32),
-        ],
+            pltpu.VMEM((BLK, CYC, 256), BF16),
+            pltpu.VMEM((BLK, CYC, 256), BF16),
+            pltpu.SemaphoreType.DMA((5,)),
+        ],
+        compiler_params=pltpu.CompilerParams(collective_id=0, has_side_effects=True),
         name="longitude",
-    )(flip, me, shift, vis, msg)
+    )(me, shift, vis, msg)
+
+
+def gather_kernel(part_ref, out_ref, got, sems):
+    here = lax.axis_index("shell")
+    barrier = pltpu.get_barrier_semaphore()
+    for i in range(1, SHELLS):
+        pl.semaphore_signal(barrier, inc=1, device_id={"shell": lax.rem(here + i, SHELLS)}, device_id_type=MESH)
+    pl.semaphore_wait(barrier, SHELLS - 1)
+    copies = []
+    for i in range(1, SHELLS):
+        peer = lax.rem(here + i, SHELLS)
+        copy = pltpu.make_async_remote_copy(
+            src_ref=part_ref.at[peer], dst_ref=got.at[i - 1], send_sem=sems.at[0, i - 1], recv_sem=sems.at[1, i - 1],
+            device_id={"shell": peer}, device_id_type=MESH,
+        )
+        copy.start()
+        copies.append(copy)
+    for copy in copies:
+        copy.wait()
+    for c in range(COMPS):
+        total = part_ref[here, c].astype(F32)
+        for i in range(SHELLS - 1):
+            total = total + got[i, c].astype(F32)
+        out_ref[c] = total
+
+
+def run_gather(part):
+    whole = pl.BlockSpec(memory_space=pltpu.VMEM)
+    shape = (COMPS, ORDERS, PARTS, DEG // SHELLS)
+    return pl.pallas_call(
+        gather_kernel,
+        in_specs=[whole],
+        out_specs=whole,
+        out_shape=jax.ShapeDtypeStruct(shape, F32),
+        scratch_shapes=[pltpu.VMEM((SHELLS - 1,) + shape, BF16), pltpu.SemaphoreType.DMA((2, SHELLS - 1))],
+        compiler_params=pltpu.CompilerParams(collective_id=1, has_side_effects=True),
+        name="gather",
+    )(part)
 
 
 def analysis_kernel(ord_ref, rad_ref, lat_ref, tab_ref, msg_ref, out_ref, sum_ref, side):
@@ -327,12 +421,15 @@
     scaled = coef * rad_ref[0]
     for c in range(COMPS):
         out_ref[c, slot] = coef[2 * c : 2 * c + 2].astype(BF16)
-        sum_ref[c, slot] = scaled[2 * c : 2 * c + 2].astype(BF16)
+        for i in range(SHELLS):
+            share = DEG // SHELLS
+            sum_ref[i, c, slot] = scaled[2 * c : 2 * c + 2, i * share : (i + 1) * share].astype(BF16)
 
 
 def run_analysis(my_orders, rad, lat, tab, msg):
     full = lambda shape: pl.BlockSpec(shape, lambda i: (0,) * len(shape))
     shape = (COMPS, ORDERS, PARTS, DEG)
+    split = (SHELLS, COMPS, ORDERS, PARTS, DEG // SHELLS)
     return pl.pallas_call(
         analysis_kernel,
         grid=(ORDERS,),
@@ -343,8 +440,8 @@
             pl.BlockSpec((1, DEG, HALF), lambda i: (i, 0, 0)),
             full((BLK, CYC, 256)),
         ],
-        out_specs=[full(shape), full(shape)],
-        out_shape=[jax.ShapeDtypeStruct(shape, BF16)] * 2,
+        out_specs=[full(shape), full(split)],
+        out_shape=[jax.ShapeDtypeStruct(shape, BF16), jax.ShapeDtypeStruct(split, BF16)],
         scratch_shapes=[pltpu.VMEM((TILES, 2, 256, 128), F32)],
         name="analysis",
     )(my_orders, rad, lat, tab, msg)
@@ -373,13 +470,9 @@
     my_orders = lax.dynamic_slice_in_dim(order_map, index * ORDERS, ORDERS)
     me, mb = order_columns(order_map, index)
     tab, msg = run_legendre(my_orders, mb, lat, g, strain_spec.reshape(COMPS, ORDERS, PARTS, DEG))
-    msg = lax.all_to_all(msg, "blk", split_axis=0, concat_axis=0, tiled=True)
-    flip = (index >= BLK // 2).astype(jnp.int32).reshape(1)
-    msg = run_longitude(flip, me, jnp.asarray(shift_table()), viscosity.reshape(CYC, POINTS), msg)
-    msg = lax.all_to_all(msg, "blk", split_axis=0, concat_axis=0, tiled=True)
+    msg = run_longitude(me, jnp.asarray(shift_table()), viscosity.reshape(CYC, POINTS), msg)
     spec, part = run_analysis(my_orders, radial_weight, lat, tab, msg)
-    summed = lax.psum_scatter(part, "shell", scatter_dimension=3, tiled=True)
-    return spec.reshape(strain_spec.shape), summed.astype(F32)
+    return spec.reshape(strain_spec.shape), run_gather(part)
 
 
 def solution(mesh):

time: 270 us -> 118 us (0.44)
  the two profiles are of different devices: /device:TPU:1 before, /device:TPU:97 now
where the time goes in v2:
time: 118 us; the launch traced here: 117 us
  Pallas kernels  110 us (93%)
  local copies, waits for them, and re-layouts  5.75 us (5%)
  between operations  1.33 us (1%)
    pallas_call x1, Pallas kernels, run_longitude(): pl.pallas_call(longitude_kernel, in_specs=[whole] * 4, out_specs=pl.Block...  40.5 us
    pallas_call x1, Pallas kernels, run_legendre(): pl.pallas_call(legendre_kernel, grid=(DEG // LB,), in_specs=[pl.BlockSpec...  35.6 us
    pallas_call x1, Pallas kernels, run_gather(): pl.pallas_call(gather_kernel, in_specs=[whole], out_specs=whole, out_shap...  17.9 us
    pallas_call x1, Pallas kernels, run_analysis(): pl.pallas_call(analysis_kernel, grid=(ORDERS,), in_specs=[pl.BlockSpec(me...  15.8 us

profile of v2, /device:TPU:97, one launch (start us, length us, event | category | flops | bytes accessed | tf_op | source)
XLA Modules:
  0.0 117.0 jit_solution(17612062449429688502)
XLA Ops:
  1.3 1.3 %dynamic_slice.6.ord_ref = s32[16]{0:T(128)} dynamic-slice(s32[1024]{0:T(1024)} %param.8, s32[]{:T(128)S(6)} %select_n.29), dynamic_slice_sizes={16} | dynamic-slice | bytes 132 | tf_op jit(solution)/shard_map/dynamic_slice | solution.py:470
  2.6 0.9 reshape.49
  3.4 0.3 slice_reduce_fusion
  3.8 0.1 dynamic-slice_bitcast_fusion
  3.9 0.7 broadcast_in_dim.4.mb_ref
  4.5 0.1 squeeze.14
  4.6 0.1 squeeze.13
  4.7 0.8 broadcast_in_dim.5.me_ref
  5.6 35.6 %legendre.1 = (bf16[16,1024,512]{2,1,0:T(8,128)(2,1)}, bf16[64,16,256]{2,1,0:T(8,128)(2,1)}) custom-call(s32[16]{0:T(128)} %dynamic_slice.6.ord_ref, f32[2,8,128]{2,1,0:T(8,128)} %broadcast_in_dim.4.mb_ref, f32[8,512]{1,0:T(8,128)} %constant.39.clone.lat_ref, f32[1,1024]{1,0:T(1,128)} %constant.40.clone.g_ref, bf16[6,16,2,1024]{3,2,1,0:T(2,128)(2,1)} %bitcast.9), custom_call_target="tpu_custom_call" | custom-call | tf_op jit(solution)/shard_map/legendre/pallas_call | solution.py:162
  41.2 40.5 %longitude.1.msg_ref = bf16[64,16,256]{2,1,0:T(8,128)(2,1)} custom-call(f32[64,8,128]{2,1,0:T(8,128)} %broadcast_in_dim.5.me_ref, f32[2,1024]{1,0:T(2,128)} %constant.41.clone.shift_ref, f32[16,2048]{1,0:T(8,128)} %bitcast.10, bf16[64,16,256]{2,1,0:T(8,128)(2,1)} %get-tuple-element.7.msg_ref), custom_call_target="tpu_custom_call" | custom-call | tf_op jit(solution)/shard_map/longitude/pallas_call | solution.py:336
  81.7 15.8 %analysis.1 = (bf16[6,16,2,1024]{3,2,1,0:T(2,128)(2,1)}, bf16[4,6,16,2,256]{4,3,2,1,0:T(2,128)(2,1)}) custom-call(s32[16]{0:T(128)} %dynamic_slice.6.ord_ref, f32[1]{0:T(128)S(6)} %copy.13.rad_ref, f32[8,512]{1,0:T(8,128)} %constant.39.clone.lat_ref, bf16[16,1024,512]{2,1,0:T(8,128)(2,1)} %get-tuple-element.6.tab_ref, bf16[64,16,256]{2,1,0:T(8,128)(2,1)} %longitude.1.msg_ref), custom_call_target="tpu_custom_call" | custom-call | tf_op jit(solution)/shard_map/analysis/pallas_call | solution.py:433
  97.5 17.9 %gather.1 = f32[6,16,2,256]{3,2,1,0:T(2,128)} custom-call(bf16[4,6,16,2,256]{4,3,2,1,0:T(2,128)(2,1)} %get-tuple-element.9.part_ref), custom_call_target="tpu_custom_call" | custom-call | tf_op jit(solution)/shard_map/gather/pallas_call | solution.py:383
  115.4 1.6 %copy.14 = f32[6,16,2,256]{3,2,1,0:T(2,128)} copy(f32[6,16,2,256]{3,2,1,0:T(2,128)} %gather.1) | data formatting | bytes 393216
  (3 shorter events, 0.0 us)

commit v3 on v2

v3 whole, which is shorter than its diff:
```python
import functools
import math

import jax
import jax.numpy as jnp
import numpy as np
from jax import lax
from jax.experimental import pallas as pl
from jax.experimental.pallas import tpu as pltpu
from jax.sharding import PartitionSpec as P

F32 = jnp.float32
BF16 = jnp.bfloat16
COMPS = 6
PARTS = 2
ORDERS = 16
DEG = 1024
HALF = 512
BLK = 64
SHELLS = 4
CYC = 16
POINTS = 2048
KH = POINTS // 2
LB = 256
LSTRIDE = LB + 1
TILES = HALF // 128
PAIRS = 8
STEPS = DEG // LB + 1
TURN = 16
TURNS = LB // TURN
BIG = 2.0**40
SMALL = 2.0**-40
NT = (((1,), (1,)), ((), ()))
MESH = pl.DeviceIdType.MESH


def latitude_constants():
    j = np.arange(HALF, dtype=np.float64)
    theta = np.pi * (2.0 * j + 1.0) / (4.0 * HALF)
    x = np.cos(theta)
    logsin = np.log2(np.sin(theta))
    hi = np.round(logsin * 512.0) / 512.0
    lo = logsin - hi
    k = np.arange(1, HALF + 1, dtype=np.float64)
    phase = np.outer(k, 2.0 * j + 1.0) % (4.0 * HALF)
    series = np.sum(np.cos(phase * np.pi / (2.0 * HALF)) / (4.0 * k * k - 1.0)[:, None], axis=0)
    weight = (2.0 / (2.0 * HALF)) * (1.0 - 2.0 * series)
    m = np.arange(DEG, dtype=np.float64)
    fac = np.concatenate([[0.0], np.cumsum(np.log2(1.0 - 0.5 / np.arange(1, DEG)))])
    g = 0.5 * np.log2((2.0 * m + 1.0) / (4.0 * np.pi)) + 0.5 * fac
    lat = np.stack([x, hi, lo, weight]).astype(np.float32)
    return np.concatenate([lat, np.zeros((4, HALF), np.float32)]), g.astype(np.float32)[None]


def power_of(e):
    return jnp.where(e < -126.0, 0.0, jnp.exp(jnp.maximum(e, -126.0) * math.log(2.0)))


def legendre_kernel(ord_ref, lat_ref, g_ref, spec_ref, tab_ref, tail_ref, msg_ref, ca, cab, prev, cur, expo, ini, ini2, expo2, scale2, mark, bca, bcb, ft, acc, lhs, lt, tailb, ns, flag):
    step = pl.program_id(0)
    base = lax.axis_index("blk") * ORDERS
    sub8 = lax.broadcasted_iota(jnp.int32, (8, 128), 0)

    @pl.when(step == 0)
    def _():
        def clear(i, _):
            flag[i] = 0
            return 0

        lax.fori_loop(0, STEPS * PAIRS, clear, 0)
        flag[0] = 1
        even = jnp.zeros((8, 128), jnp.int32)
        for p in range(PAIRS):
            first = ord_ref[base + 2 * p]
            e = jnp.where((first & 1) == 0, first, DEG - 1 - first)
            even = jnp.where(sub8 == p, e, even)
            flag[(DEG - e) // (2 * TURN)] = 1
        ma = even.astype(F32)
        mb = (DEG - 1.0) - ma
        mark[...] = mb + 1.0
        lane = lax.broadcasted_iota(jnp.int32, (8, 128), 1).astype(F32)
        for b in range(STEPS * LB // 128 + 1):
            t = lane + float(128 * b)
            second = t > mb
            m = jnp.where(second, mb, ma)
            l = jnp.where(second, t - 1.0, t + ma)
            up = (l > m) & (t < DEG + 0.5)
            a2 = (4.0 * l * l - 1.0) / jnp.where(up, (l - m) * (l + m), 1.0)
            a = jnp.where(up, jnp.sqrt(jnp.where(up, a2, 1.0)), 0.0)
            below = l - 1.0
            top = jnp.where(below > m, (below - m) * (below + m), 0.0)
            ab = a * jnp.sqrt(top / jnp.maximum(4.0 * below * below - 1.0, 1.0))
            for k in range(128 // TURN):
                ca[b * (128 // TURN) + k] = pltpu.roll(a, (128 - TURN * k) % 128, 1)
                cab[b * (128 // TURN) + k] = pltpu.roll(ab, (128 - TURN * k) % 128, 1)
        glane = lax.broadcasted_iota(jnp.int32, (8, DEG), 1).astype(F32)
        for m, first, power in ((ma, ini, expo), (mb, ini2, expo2)):
            gm = jnp.sum(jnp.where(glane == m[:, :1], g_ref[...], 0.0), axis=1, keepdims=True)
            for t in range(TILES):
                cols = pl.ds(128 * t, 128)
                mh = m * lat_ref[1:2, cols]
                whole = jnp.floor(mh)
                first[t] = jnp.exp(((mh - whole) + m * lat_ref[2:3, cols] + gm) * math.log(2.0))
                power[t] = whole
        for r in range(TURN):
            bca[r, 0] = jnp.broadcast_to(ca[0][:, r : r + 1], (8, 128))
            bca[r, 1] = jnp.broadcast_to(cab[0][:, r : r + 1], (8, 128))
        for t in range(TILES):
            scale2[t] = power_of(expo2[t])
            prev[t] = jnp.zeros((8, 128), F32)
            cur[t] = jnp.zeros((8, 128), F32)

        pos = lax.broadcasted_iota(jnp.int32, (16, DEG), 1)
        pos_even = (pos & 1) == 0
        narrow = lax.broadcasted_iota(jnp.int32, (16, 128), 1)

        def place(p, _):
            first = ord_ref[base + 2 * p]
            odd_first = first & 1
            e = jnp.where(odd_first == 0, first, DEG - 1 - first)
            pads = [jnp.zeros((4, DEG), F32)]
            da = jnp.concatenate([spec_ref[c, 0, 2 * p + odd_first].astype(F32) for c in range(COMPS)] + pads, axis=0)
            db = jnp.concatenate([spec_ref[c, 0, 2 * p + 1 - odd_first].astype(F32) for c in range(COMPS)] + pads, axis=0)
            da = da * jnp.where(e == 0, 1.0, 2.0)
            db = db * 2.0
            last = jnp.broadcast_to(db[:, DEG - 1 : DEG], (16, 128))
            lt[pl.ds(pl.multiple_of(16 * p, 16), 16), :] = jnp.where(narrow == p, last, 0.0).astype(BF16)
            da = pltpu.roll(da, jnp.where(e == 0, 0, DEG - e), 1)
            db = pltpu.roll(db, 1, 1)
            da = jnp.where(pos < DEG - e, da, 0.0)
            db = jnp.where(pos >= DEG - e, db, 0.0)
            lhs[p, 0:16] = jnp.where(pos_even, da, 0.0).astype(BF16)
            lhs[p, 16:32] = jnp.where(pos_even, 0.0, da).astype(BF16)
            lhs[p, 32:48] = jnp.where(pos_even, db, 0.0).astype(BF16)
            lhs[p, 48:64] = jnp.where(pos_even, 0.0, db).astype(BF16)
            return 0

        lax.fori_loop(0, PAIRS, place, 0)

    @pl.when(step == 1)
    def _():
        acc[...] = jnp.zeros_like(acc)

    new_half, old_half = lax.rem(step, 2), lax.rem(step + 1, 2)
    back = jnp.maximum(step - 1, 0)

    def advance(i, starts):
        rows = pl.ds(i * LSTRIDE, LB)
        left = lhs[i, :, pl.ds(pl.multiple_of(back * LB, LB), LB)]
        for half in range(2):
            table = jnp.concatenate([ft[old_half, 2 * half, rows, :], ft[old_half, 2 * half + 1, rows, :]], axis=1).astype(BF16)
            tab_ref[i, :, 256 * half : 256 * half + 256] = table
            acc[i, half] += jnp.dot(left, table, preferred_element_type=F32)

        xs = [jnp.broadcast_to(lat_ref[0:1, pl.ds(128 * t, 128)], (8, 128)) for t in range(TILES)]
        ps, cs, scales = [prev[t] for t in range(TILES)], [cur[t] for t in range(TILES)], [None] * TILES
        es = [expo[t] for t in range(TILES)]
        for k in range(2):
            use, make = (bca, bcb) if k == 0 else (bcb, bca)
            chunk = step * TURNS + 2 * i + k
            av, abv = ca[chunk + 1], cab[chunk + 1]
            for r in range(TURN):
                if r % 8 == 0:
                    for t in range(TILES):
                        big = jnp.abs(cs[t]) > BIG
                        f = jnp.where(big, SMALL, 1.0)
                        es[t] = jnp.where(big, es[t] + 40.0, es[t])
                        scales[t] = power_of(es[t])
                        ps[t], cs[t] = ps[t] * f, cs[t] * f
                make[r, 0] = jnp.broadcast_to(av[:, r : r + 1], (8, 128))
                make[r, 1] = jnp.broadcast_to(abv[:, r : r + 1], (8, 128))
                a, ab = use[r, 0], use[r, 1]
                if starts:
                    now = (chunk * TURN + r).astype(F32)
                    hit = mark[...] == now
                for t in range(TILES):
                    new = (a * xs[t]) * cs[t] - ab * ps[t]
                    if starts:
                        new = jnp.where(hit, ini2[t], new)
                        es[t] = jnp.where(hit, expo2[t], es[t])
                        scales[t] = jnp.where(hit, scale2[t], scales[t])
                        if r == 0 and k == 0:
                            new = jnp.where(jnp.full((8, 128), now) == 0.0, ini[t], new)
                    ps[t], cs[t] = cs[t], new
                    ft[new_half, t, pl.ds(2 * TURN * i + TURN * k + r, 8, stride=LSTRIDE), :] = new * scales[t]
        for t in range(TILES):
            prev[t], cur[t], expo[t] = ps[t], cs[t], es[t]

    def body(i, _):
        starting = flag[step * PAIRS + i] == 1

        @pl.when(starting)
        def _():
            advance(i, True)

        @pl.when(jnp.logical_not(starting))
        def _():
            advance(i, False)

        return 0

    lax.fori_loop(0, PAIRS, body, 0)

    @pl.when(step == STEPS - 1)
    def _():
        tail = jnp.concatenate([ft[new_half, t, pl.ds(0, 8, stride=LSTRIDE), :] for t in range(TILES)], axis=1)
        tailb[...] = jnp.concatenate([tail, jnp.zeros((8, HALF), F32)], axis=0).astype(BF16)
        tail_ref[...] = tailb[...]

        def spread(p, _):
            extra = jnp.dot(lt[pl.ds(pl.multiple_of(16 * p, 16), 16), 0:16], tailb[...], preferred_element_type=F32)
            for t in range(TILES):
                cols = slice(128 * (t % 2), 128 * (t % 2) + 128)
                part = acc[p, t // 2]
                for par in range(2):
                    sym, anti = part[32 * par : 32 * par + 16, cols], part[32 * par + 16 : 32 * par + 32, cols]
                    if par:
                        sym = sym + extra[:, 128 * t : 128 * t + 128]
                    ns[t, pl.ds(par * 8 + p, 16, stride=16), :] = sym + anti
                    ns[TILES + t, pl.ds(par * 8 + p, 16, stride=16), :] = sym - anti
            return 0

        lax.fori_loop(0, PAIRS, spread, 0)
        lane = lax.broadcasted_iota(jnp.int32, (8, 128), 1)
        for t in range(2 * TILES):
            near, far = ns[t, 0:128].T, ns[t, 128:256].T
            moved = pltpu.roll(far, 64, 1)
            for b in range(8):
                d = (t % TILES) * 8 + b
                dest = d if t < TILES else BLK - 1 - d
                msg_ref[dest, 0:16] = near[16 * b : 16 * b + 16].astype(BF16)
                msg_ref[dest, 16:24] = jnp.where(lane < 64, far[16 * b : 16 * b + 8], moved[16 * b + 8 : 16 * b + 16]).astype(BF16)


def run_legendre(order_map, lat, g, spec):
    full = lambda shape: pl.BlockSpec(shape, lambda i: (0,) * len(shape))
    return pl.pallas_call(
        legendre_kernel,
        grid=(STEPS,),
        in_specs=[
            pl.BlockSpec(memory_space=pltpu.SMEM),
            full((8, HALF)),
            full((1, DEG)),
            full((COMPS, 1, ORDERS, PARTS, DEG)),
        ],
        out_specs=[
            pl.BlockSpec((PAIRS, LB, HALF), lambda i: (0, jnp.maximum(i - 1, 0), 0)),
            full((16, HALF)),
            full((BLK, 24, 128)),
        ],
        out_shape=[
            jax.ShapeDtypeStruct((PAIRS, DEG, HALF), BF16),
            jax.ShapeDtypeStruct((16, HALF), BF16),
            jax.ShapeDtypeStruct((BLK, 24, 128), BF16),
        ],
        scratch_shapes=[
            pltpu.VMEM((STEPS * TURNS + 128 // TURN, 8, 128), F32),
            pltpu.VMEM((STEPS * TURNS + 128 // TURN, 8, 128), F32),
            pltpu.VMEM((TILES, 8, 128), F32),
            pltpu.VMEM((TILES, 8, 128), F32),
            pltpu.VMEM((TILES, 8, 128), F32),
            pltpu.VMEM((TILES, 8, 128), F32),
            pltpu.VMEM((TILES, 8, 128), F32),
            pltpu.VMEM((TILES, 8, 128), F32),
            pltpu.VMEM((TILES, 8, 128), F32),
            pltpu.VMEM((8, 128), F32),
            pltpu.VMEM((TURN, 2, 8, 128), F32),
            pltpu.VMEM((TURN, 2, 8, 128), F32),
            pltpu.VMEM((2, TILES, PAIRS * LSTRIDE + 8, 128), F32),
            pltpu.VMEM((PAIRS, 2, 64, 256), F32),
            pltpu.VMEM((PAIRS, 64, DEG), BF16),
            pltpu.VMEM((128, 128), BF16),
            pltpu.VMEM((16, HALF), BF16),
            pltpu.VMEM((2 * TILES, 256, 128), F32),
            pltpu.SMEM((STEPS * PAIRS,), jnp.int32),
        ],
        name="legendre",
    )(order_map, lat, g, spec)


def turn(phase):
    t = phase * (1.0 / KH) - 1.0
    z = t * t
    c = jnp.full_like(z, 0.0)
    s = jnp.full_like(z, 0.0)
    for i in range(8, -1, -1):
        c = c * z + float((-1) ** (i + 1) * math.pi ** (2 * i) / math.factorial(2 * i))
        s = s * z + float((-1) ** (i + 1) * math.pi ** (2 * i + 1) / math.factorial(2 * i + 1))
    return c, s * t


def wrap(value):
    return value - POINTS * jnp.floor(value * (1.0 / POINTS))


def turned(value, quarters):
    return pltpu.roll(value, (32 * quarters) % 128, 1) if quarters % 4 else value


def longitude_kernel(ord_ref, shift_ref, vis_ref, msg_ref, out_ref, wave, left, pm, spect, vis, got, give, sems):
    here = lax.axis_index("blk")
    barrier = pltpu.get_barrier_semaphore()

    def greet(i, _):
        pl.semaphore_signal(barrier, inc=1, device_id={"blk": lax.rem(here + i, BLK)}, device_id_type=MESH)
        return 0

    lax.fori_loop(1, BLK, greet, 0)
    pl.semaphore_wait(barrier, BLK - 1)

    def first_copy(peer, mine):
        return pltpu.make_async_remote_copy(
            src_ref=msg_ref.at[peer], dst_ref=got.at[mine], send_sem=sems.at[0], recv_sem=sems.at[1],
            device_id={"blk": peer}, device_id_type=MESH,
        )

    def send_first(i, _):
        first_copy(lax.rem(here + i, BLK), here).start()
        return 0

    lax.fori_loop(1, BLK, send_first, 0)
    own = pltpu.make_async_copy(msg_ref.at[here], got.at[here], sems.at[4])
    own.start()

    lane = lax.broadcasted_iota(jnp.int32, (8, 128), 1).astype(F32)
    sub8 = lax.broadcasted_iota(jnp.int32, (8, 128), 0)
    sc, ss = [], []
    for u in range(KH // 128):
        sc.append(jnp.broadcast_to(shift_ref[0:1, pl.ds(128 * u, 128)], (8, 128)))
        ss.append(jnp.broadcast_to(shift_ref[1:2, pl.ds(128 * u, 128)], (8, 128)))

    def make(src, _):
        even = jnp.zeros((8, 128), jnp.int32)
        for p in range(PAIRS):
            first = ord_ref[src * ORDERS + 2 * p]
            even = jnp.where(sub8 == p, jnp.where((first & 1) == 0, first, DEG - 1 - first), even)
        m = even.astype(F32)
        c, s = turn(wrap(m * lane))
        gc, gs = turn(wrap(m * 128.0))
        for u in range(KH // 128):
            oc = sc[u] * c - ss[u] * s
            os = -(ss[u] * c + sc[u] * s)
            rows = pl.ds(pl.multiple_of(src * 32, 32), 32)
            wave[rows, pl.ds(128 * u, 128)] = jnp.concatenate([c, oc, -s, -os], axis=0).astype(BF16)
            c, s = c * gc - s * gs, s * gc + c * gs
        return 0

    lax.fori_loop(0, BLK, make, 0)

    for j in range(CYC):
        row = jnp.where(here >= BLK // 2, CYC - 1 - j, j)
        vis[j : j + 1, :] = vis_ref[0, pl.ds(row, 1), :]

    own.wait()
    pltpu.make_async_remote_copy(
        src_ref=msg_ref.at[0 : BLK - 1], dst_ref=got.at[0 : BLK - 1], send_sem=sems.at[0], recv_sem=sems.at[1],
        device_id={"blk": here}, device_id_type=MESH,
    ).wait()

    wide = lax.broadcasted_iota(jnp.int32, (16, 128), 1)
    even = ((wide // 8) % 2) == 0
    quarter = wide // 32
    for g in range(BLK // 4):
        pieces = [(got[4 * g + i, 0:16].astype(F32), got[4 * g + i, 16:24].astype(F32)) for i in range(4)]
        for c in range(COMPS):
            total = None
            for i in range(4):
                near, far = pieces[i]
                moved = turned(near, i - c) if c < 4 else jnp.concatenate([turned(far, i - c), turned(far, i - c - 2)], axis=0)
                total = moved if total is None else jnp.where(quarter == i, moved, total)
            left[16 * c : 16 * c + 16, pl.ds(128 * g, 128)] = jnp.where(even, total, 0.0).astype(BF16)
            left[96 + 16 * c : 112 + 16 * c, pl.ds(128 * g, 128)] = jnp.where(even, 0.0, total).astype(BF16)

    for u in range(KH // 256):
        cols = pl.ds(256 * u, 256)
        field = jnp.dot(left[...], wave[:, cols], preferred_element_type=F32)
        low, high = vis[:, cols], vis[:, pl.ds(KH + 256 * u, 256)]
        for c in range(COMPS):
            e, o = field[16 * c : 16 * c + 16], field[96 + 16 * c : 112 + 16 * c]
            first, second = low * (e + o), high * (e - o)
            pm[16 * c : 16 * c + 16, cols] = (first + second).astype(BF16)
            pm[96 + 16 * c : 112 + 16 * c, cols] = (first - second).astype(BF16)

    def back(b, _):
        rows = pl.ds(pl.multiple_of(b * 256, 256), 256)
        both = lax.dot_general(pm[...], wave[rows, :], NT, preferred_element_type=F32)
        lanes = lax.broadcasted_iota(jnp.int32, (96, 256), 1)
        pick = ((lanes // 8) % 2) == 0
        spect[:, rows] = jnp.where(pick, both[:96], both[96:]) * (2.0 * math.pi / POINTS)
        return 0

    lax.fori_loop(0, POINTS // 256, back, 0)

    def pack(g, _):
        cols = pl.ds(pl.multiple_of(g * 128, 128), 128)
        vals = [spect[16 * c : 16 * c + 16, cols] for c in range(COMPS)]
        for i in range(4):
            near = None
            for c in range(4):
                moved = turned(vals[c], c - i)
                near = moved if near is None else jnp.where(quarter == c, moved, near)
            far = None
            for c in range(4):
                moved = turned(vals[4 + c % 2][8 * (c // 2) : 8 * (c // 2) + 8], c - i)
                far = moved if far is None else jnp.where(quarter[:8] == c, moved, far)
            give[4 * g + i, 0:16] = near.astype(BF16)
            give[4 * g + i, 16:24] = far.astype(BF16)
        return 0

    lax.fori_loop(0, BLK // 4, pack, 0)

    def send_second(i, _):
        peer = lax.rem(here + i, BLK)
        pltpu.make_async_remote_copy(
            src_ref=give.at[peer], dst_ref=out_ref.at[here], send_sem=sems.at[2], recv_sem=sems.at[3],
            device_id={"blk": peer}, device_id_type=MESH,
        ).start()
        return 0

    lax.fori_loop(1, BLK, send_second, 0)
    own = pltpu.make_async_copy(give.at[here], out_ref.at[here], sems.at[4])
    own.start()
    own.wait()
    pltpu.make_async_remote_copy(
        src_ref=give.at[0 : BLK - 1], dst_ref=out_ref.at[0 : BLK - 1], send_sem=sems.at[2], recv_sem=sems.at[3],
        device_id={"blk": here}, device_id_type=MESH,
    ).wait()


def run_longitude(order_map, shift, vis, msg):
    whole = pl.BlockSpec(memory_space=pltpu.VMEM)
    return pl.pallas_call(
        longitude_kernel,
        in_specs=[pl.BlockSpec(memory_space=pltpu.SMEM)] + [whole] * 3,
        out_specs=pl.BlockSpec(memory_space=pl.ANY),
        out_shape=jax.ShapeDtypeStruct((BLK, 24, 128), BF16),
        scratch_shapes=[
            pltpu.VMEM((POINTS, KH), BF16),
            pltpu.VMEM((192, POINTS), BF16),
            pltpu.VMEM((192, KH), BF16),
            pltpu.VMEM((96, POINTS), F32),
            pltpu.VMEM((CYC, POINTS), F32),
            pltpu.VMEM((BLK, 24, 128), BF16),
            pltpu.VMEM((BLK, 24, 128), BF16),
            pltpu.SemaphoreType.DMA((5,)),
        ],
        compiler_params=pltpu.CompilerParams(collective_id=0, has_side_effects=True),
        name="longitude",
    )(order_map, shift, vis, msg)


def gather_kernel(part_ref, out_ref, near, total, give, far, sems):
    here = lax.axis_index("shell")
    layer, core = here // 2, lax.rem(here, 2)
    partner, across = 2 * layer + 1 - core, 2 * (1 - layer) + core
    barrier = pltpu.get_barrier_semaphore()
    for peer in (partner, across):
        pl.semaphore_signal(barrier, inc=1, device_id={"shell": peer}, device_id_type=MESH)
    pl.semaphore_wait(barrier, 2)
    first = []
    for c in range(COMPS):
        for k in range(2):
            share = 2 * (1 - layer if k == 0 else layer) + 1 - core
            copy = pltpu.make_async_remote_copy(
                src_ref=part_ref.at[share, c], dst_ref=near.at[k, c], send_sem=sems.at[0, k, c], recv_sem=sems.at[1, k, c],
                device_id={"shell": partner}, device_id_type=MESH,
            )
            copy.start()
            first.append(copy)
    second = []
    for c in range(COMPS):
        first[2 * c].wait_recv()
        give[c] = (part_ref[across, c].astype(F32) + near[0, c].astype(F32)).astype(BF16)
        copy = pltpu.make_async_remote_copy(
            src_ref=give.at[c], dst_ref=far.at[c], send_sem=sems.at[2, 0, c], recv_sem=sems.at[2, 1, c],
            device_id={"shell": across}, device_id_type=MESH,
        )
        copy.start()
        second.append(copy)
    for c in range(COMPS):
        first[2 * c + 1].wait_recv()
        total[c] = part_ref[here, c].astype(F32) + near[1, c].astype(F32)
    for c in range(COMPS):
        second[c].wait_recv()
        out_ref[c] = total[c] + far[c].astype(F32)
    for copy in first + second:
        copy.wait_send()


def run_gather(part):
    whole = pl.BlockSpec(memory_space=pltpu.VMEM)
    shape = (COMPS, ORDERS, PARTS, DEG // SHELLS)
    return pl.pallas_call(
        gather_kernel,
        in_specs=[whole],
        out_specs=whole,
        out_shape=jax.ShapeDtypeStruct(shape, F32),
        scratch_shapes=[
            pltpu.VMEM((2,) + shape, BF16),
            pltpu.VMEM(shape, F32),
            pltpu.VMEM(shape, BF16),
            pltpu.VMEM(shape, BF16),
            pltpu.SemaphoreType.DMA((3, 2, COMPS)),
        ],
        compiler_params=pltpu.CompilerParams(collective_id=1, has_side_effects=True),
        name="gather",
    )(part)


def analysis_kernel(ord_ref, rad_ref, lat_ref, tail_ref, tab_ref, msg_ref, out_ref, sum_ref, side):
    p = pl.program_id(0)
    base = lax.axis_index("blk") * ORDERS

    @pl.when(p == 0)
    def _():
        def fetch(d):
            near, far = msg_ref[d, 0:16].astype(F32), msg_ref[d, 16:24].astype(F32)
            return near, jnp.concatenate([far, pltpu.roll(far, 64, 1)], axis=0)

        for t in range(TILES):
            w = lat_ref[3:4, pl.ds(128 * t, 128)]
            north = [fetch(8 * t + b) for b in range(8)]
            south = [fetch(BLK - 1 - 8 * t - b) for b in range(8)]
            for h in range(2):
                lanes = pl.ds(128 * h, 128)
                up = jnp.concatenate([v[h] for v in north], axis=0)
                down = jnp.concatenate([v[h] for v in south], axis=0)
                side[t, 0, lanes, :] = (up + down).T * w
                side[t, 1, lanes, :] = (up - down).T * w

    first = ord_ref[base + 2 * p]
    odd_first = first & 1
    e = jnp.where(odd_first == 0, first, DEG - 1 - first)
    left = jnp.concatenate(
        [
            jnp.concatenate([side[t, half, pl.ds(8 * par + p, 16, stride=16), :] for t in range(TILES)], axis=1)
            for par in range(2)
            for half in range(2)
        ],
        axis=0,
    ).astype(BF16)
    both = lax.dot_general(left, tab_ref[0], NT, preferred_element_type=F32)
    final = lax.dot_general(left[32:48], tail_ref[...], NT, preferred_element_type=F32)
    final = jnp.sum(jnp.where(lax.broadcasted_iota(jnp.int32, (16, 16), 1) == p, final, 0.0), axis=1, keepdims=True)
    pos = lax.broadcasted_iota(jnp.int32, (16, DEG), 1)
    pos_even = (pos & 1) == 0
    ca = jnp.where(pos_even, both[0:16], both[16:32])
    cb = jnp.where(pos_even, both[32:48], both[48:64])
    ca = jnp.where(pos >= e, pltpu.roll(ca, e, 1), 0.0)
    cb = jnp.where(pos >= DEG - 1 - e, pltpu.roll(cb, DEG - 1, 1), 0.0)
    cb = jnp.where(pos == DEG - 1, final, cb)
    share = DEG // SHELLS
    for coef, slot in ((ca, 2 * p + odd_first), (cb, 2 * p + 1 - odd_first)):
        scaled = coef * rad_ref[0]
        for c in range(COMPS):
            out_ref[c, 0, slot] = coef[2 * c : 2 * c + 2].astype(BF16)
            for i in range(SHELLS):
                sum_ref[i, c, slot] = scaled[2 * c : 2 * c + 2, i * share : (i + 1) * share].astype(BF16)


def run_analysis(order_map, rad, lat, tail, tab, msg):
    full = lambda shape: pl.BlockSpec(shape, lambda i: (0,) * len(shape))
    shape = (COMPS, 1, ORDERS, PARTS, DEG)
    split = (SHELLS, COMPS, ORDERS, PARTS, DEG // SHELLS)
    return pl.pallas_call(
        analysis_kernel,
        grid=(PAIRS,),
        in_specs=[
            pl.BlockSpec(memory_space=pltpu.SMEM),
            pl.BlockSpec(memory_space=pltpu.SMEM),
            full((8, HALF)),
            full((16, HALF)),
            pl.BlockSpec((1, DEG, HALF), lambda i: (i, 0, 0)),
            full((BLK, 24, 128)),
        ],
        out_specs=[full(shape), full(split)],
        out_shape=[jax.ShapeDtypeStruct(shape, BF16), jax.ShapeDtypeStruct(split, BF16)],
        scratch_shapes=[pltpu.VMEM((TILES, 2, 256, 128), F32)],
        name="analysis",
    )(order_map, rad, lat, tail, tab, msg)


def shift_table():
    k = np.arange(KH, dtype=np.float64)
    ang = 2.0 * np.pi * k / POINTS
    sign = 1.0 - 2.0 * (k % 2)
    return np.stack([sign * np.cos(ang), sign * np.sin(ang)]).astype(np.float32)


def shards(strain_spec, order_map, viscosity, radial_weight):
    lat, g = latitude_constants()
    lat, g = jnp.asarray(lat), jnp.asarray(g)
    tab, tail, msg = run_legendre(order_map, lat, g, strain_spec)
    msg = run_longitude(order_map, jnp.asarray(shift_table()), viscosity, msg)
    spec, part = run_analysis(order_map, radial_weight, lat, tail, tab, msg)
    return spec, run_gather(part)


def solution(mesh):
    return jax.shard_map(
        shards,
        mesh=mesh,
        in_specs=(P(None, "shell", "blk", None, None), P(), P("shell", "blk", None), P("shell")),
        out_specs=(P(None, "shell", "blk", None, None), P(None, "blk", None, "shell")),
        check_vma=False,
    )
```

time: 118 us -> 77.8 us (0.66)
  Pallas kernels: 110 us -> 74.6 us
  local copies, waits for them, and re-layouts: 5.75 us -> 1.62 us
    pallas_call x3, Pallas kernels: 91.9 us -> 60.1 us  [the longest x1 35.8 us: run_longitude(): pl.pallas_call(longitude_kernel, in_specs=[pl.BlockSpec(memory_space=pltp...]
    pallas_call x1, Pallas kernels: 17.9 us -> 14.4 us  [run_gather(): pl.pallas_call(gather_kernel, in_specs=[whole], out_specs=whole, out_shap...]
    broadcast_in_dim x2 -> x0, local copies, waits for them, and re-layouts: 1.51 us -> none  [the longest x1 0.84 us: order_columns(): me = jnp.broadcast_to(evens.reshape(BLK, 8, 1), (BLK, 8, 128))]
    dynamic_slice x1 -> x0, local copies, waits for them, and re-layouts: 1.28 us -> none  [shards(): my_orders = lax.dynamic_slice_in_dim(order_map, index * ORDERS, ORDERS)]
where the time goes in v3:
time: 77.8 us; the launch traced here: 77.5 us
  Pallas kernels  74.6 us (96%)
  local copies, waits for them, and re-layouts  1.62 us (2%)
  between operations  1.29 us (2%)
    pallas_call x1, Pallas kernels, run_longitude(): pl.pallas_call(longitude_kernel, in_specs=[pl.BlockSpec(memory_space=pltp...  35.8 us
    pallas_call x1, Pallas kernels, run_legendre(): pl.pallas_call(legendre_kernel, grid=(STEPS,), in_specs=[pl.BlockSpec(mem...  14.8 us
    pallas_call x1, Pallas kernels, run_gather(): pl.pallas_call(gather_kernel, in_specs=[whole], out_specs=whole, out_shap...  14.4 us
    pallas_call x1, Pallas kernels, run_analysis(): pl.pallas_call(analysis_kernel, grid=(PAIRS,), in_specs=[pl.BlockSpec(mem...  9.46 us
    unnamed x1, local copies, waits for them, and re-layouts  1.62 us

profile of v3, /device:TPU:97, one launch (start us, length us, event | category | flops | bytes accessed | tf_op | source)
XLA Modules:
  0.0 77.5 jit_solution(2114427030765473400)
XLA Ops:
  1.3 14.8 %legendre.1 = (bf16[8,1024,512]{2,1,0:T(8,128)(2,1)}, bf16[16,512]{1,0:T(8,128)(2,1)}, bf16[64,24,128]{2,1,0:T(8,128)(2,1)}) custom-call(s32[1024]{0:T(1024)} %ord_ref.5, f32[8,512]{1,0:T(8,128)} %constant.6.clone.lat_ref, f32[1,1024]{1,0:T(1,128)} %constant.7.clone.g_ref, bf16[6,1,16,2,1024]{4,3,2,1,0:T(2,128)(2,1)} %spec_ref.1), custom_call_target="tpu_custom_call" | custom-call | tf_op jit(solution)/shard_map/legendre/pallas_call | solution.py:237
  16.1 35.8 %longitude.1.msg_ref = bf16[64,24,128]{2,1,0:T(8,128)(2,1)} custom-call(s32[1024]{0:T(1024)} %ord_ref.5, f32[2,1024]{1,0:T(2,128)} %constant.8.clone.shift_ref, f32[1,16,2048]{2,1,0:T(8,128)} %vis_ref.1, bf16[64,24,128]{2,1,0:T(8,128)(2,1)} %get-tuple-element.9.msg_ref), custom_call_target="tpu_custom_call" | custom-call | tf_op jit(solution)/shard_map/longitude/pallas_call | solution.py:432
  51.9 9.5 %analysis.1 = (bf16[6,1,16,2,1024]{4,3,2,1,0:T(2,128)(2,1)}, bf16[4,6,16,2,256]{4,3,2,1,0:T(2,128)(2,1)}) custom-call(s32[1024]{0:T(1024)} %ord_ref.5, f32[1]{0:T(128)S(6)} %copy.10.rad_ref, f32[8,512]{1,0:T(8,128)} %constant.6.clone.lat_ref, bf16[16,512]{1,0:T(8,128)(2,1)} %get-tuple-element.7.tail_ref, bf16[8,1024,512]{2,1,0:T(8,128)(2,1)} %get-tuple-element.8.tab_ref, ...), custom_call_target="tpu_custom_call" | custom-call | tf_op jit(solution)/shard_map/analysis/pallas_call | solution.py:565
  61.4 14.4 %gather.1 = f32[6,16,2,256]{3,2,1,0:T(2,128)} custom-call(bf16[4,6,16,2,256]{4,3,2,1,0:T(2,128)(2,1)} %get-tuple-element.11.part_ref), custom_call_target="tpu_custom_call" | custom-call | tf_op jit(solution)/shard_map/gather/pallas_call | solution.py:493
  75.9 1.6 %copy.11 = f32[6,16,2,256]{3,2,1,0:T(2,128)} copy(f32[6,16,2,256]{3,2,1,0:T(2,128)} %gather.1) | data formatting | bytes 393216

commit v4 on v3

--- a/solution.py
+++ b/solution.py
@@ -1,4 +1,3 @@
-import functools
 import math
 
 import jax
@@ -28,6 +27,7 @@
 STEPS = DEG // LB + 1
 TURN = 16
 TURNS = LB // TURN
+EARLY = 36
 BIG = 2.0**40
 SMALL = 2.0**-40
 NT = (((1,), (1,)), ((), ()))
@@ -297,8 +297,16 @@
     return pltpu.roll(value, (32 * quarters) % 128, 1) if quarters % 4 else value
 
 
-def longitude_kernel(ord_ref, shift_ref, vis_ref, msg_ref, out_ref, wave, left, pm, spect, vis, got, give, sems):
+def tail_kernel(
+    ord_ref, rad_ref, shift_ref, vis_ref, lat_ref, last_ref, msg_ref, tab_hbm, out_ref, sum_ref,
+    tab, wave, left, pm, vis, got, give, back, side, part, held, near, pass_on, far, sems, pair_sems,
+):
     here = lax.axis_index("blk")
+    shell = lax.axis_index("shell")
+    layer, core = shell // 2, lax.rem(shell, 2)
+    partner, across = 2 * layer + 1 - core, 2 * (1 - layer) + core
+    load = pltpu.make_async_copy(tab_hbm, tab, sems.at[5])
+    load.start()
     barrier = pltpu.get_barrier_semaphore()
 
     def greet(i, _):
@@ -306,21 +314,8 @@
         return 0
 
     lax.fori_loop(1, BLK, greet, 0)
-    pl.semaphore_wait(barrier, BLK - 1)
-
-    def first_copy(peer, mine):
-        return pltpu.make_async_remote_copy(
-            src_ref=msg_ref.at[peer], dst_ref=got.at[mine], send_sem=sems.at[0], recv_sem=sems.at[1],
-            device_id={"blk": peer}, device_id_type=MESH,
-        )
-
-    def send_first(i, _):
-        first_copy(lax.rem(here + i, BLK), here).start()
-        return 0
-
-    lax.fori_loop(1, BLK, send_first, 0)
-    own = pltpu.make_async_copy(msg_ref.at[here], got.at[here], sems.at[4])
-    own.start()
+    for peer in (partner, across):
+        pl.semaphore_signal(barrier, inc=1, device_id={"shell": peer}, device_id_type=MESH)
 
     lane = lax.broadcasted_iota(jnp.int32, (8, 128), 1).astype(F32)
     sub8 = lax.broadcasted_iota(jnp.int32, (8, 128), 0)
@@ -345,7 +340,21 @@
             c, s = c * gc - s * gs, s * gc + c * gs
         return 0
 
-    lax.fori_loop(0, BLK, make, 0)
+    lax.fori_loop(0, EARLY, make, 0)
+    pl.semaphore_wait(barrier, BLK + 1)
+
+    def send_first(i, _):
+        peer = lax.rem(here + i, BLK)
+        pltpu.make_async_remote_copy(
+            src_ref=msg_ref.at[peer], dst_ref=got.at[here], send_sem=sems.at[0], recv_sem=sems.at[1],
+            device_id={"blk": peer}, device_id_type=MESH,
+        ).start()
+        return 0
+
+    lax.fori_loop(1, BLK, send_first, 0)
+    own = pltpu.make_async_copy(msg_ref.at[here], got.at[here], sems.at[4])
+    own.start()
+    lax.fori_loop(EARLY, BLK, make, 0)
 
     for j in range(CYC):
         row = jnp.where(here >= BLK // 2, CYC - 1 - j, j)
@@ -365,8 +374,8 @@
         for c in range(COMPS):
             total = None
             for i in range(4):
-                near, far = pieces[i]
-                moved = turned(near, i - c) if c < 4 else jnp.concatenate([turned(far, i - c), turned(far, i - c - 2)], axis=0)
+                first, rest = pieces[i]
+                moved = turned(first, i - c) if c < 4 else jnp.concatenate([turned(rest, i - c), turned(rest, i - c - 2)], axis=0)
                 total = moved if total is None else jnp.where(quarter == i, moved, total)
             left[16 * c : 16 * c + 16, pl.ds(128 * g, 128)] = jnp.where(even, total, 0.0).astype(BF16)
             left[96 + 16 * c : 112 + 16 * c, pl.ds(128 * g, 128)] = jnp.where(even, 0.0, total).astype(BF16)
@@ -381,203 +390,196 @@
             pm[16 * c : 16 * c + 16, cols] = (first + second).astype(BF16)
             pm[96 + 16 * c : 112 + 16 * c, cols] = (first - second).astype(BF16)
 
-    def back(b, _):
-        rows = pl.ds(pl.multiple_of(b * 256, 256), 256)
+    lanes = lax.broadcasted_iota(jnp.int32, (96, 256), 1)
+    pick = ((lanes // 8) % 2) == 0
+
+    def send_block(blk):
+        for i in range(8):
+            peer = blk * 8 + i
+
+            @pl.when(peer != here)
+            def _():
+                pltpu.make_async_remote_copy(
+                    src_ref=give.at[peer], dst_ref=back.at[here], send_sem=sems.at[2], recv_sem=sems.at[3],
+                    device_id={"blk": peer}, device_id_type=MESH,
+                ).start()
+
+    def block_of(b):
+        return lax.rem(b + here // 8, 8)
+
+    def spectra(b, _):
+        blk = block_of(b)
+        rows = pl.ds(pl.multiple_of(blk * 256, 256), 256)
         both = lax.dot_general(pm[...], wave[rows, :], NT, preferred_element_type=F32)
-        lanes = lax.broadcasted_iota(jnp.int32, (96, 256), 1)
-        pick = ((lanes // 8) % 2) == 0
-        spect[:, rows] = jnp.where(pick, both[:96], both[96:]) * (2.0 * math.pi / POINTS)
+        spect = jnp.where(pick, both[:96], both[96:]) * (2.0 * math.pi / POINTS)
+        for g in range(2):
+            vals = [spect[16 * c : 16 * c + 16, 128 * g : 128 * g + 128] for c in range(COMPS)]
+            for i in range(4):
+                low = None
+                for c in range(4):
+                    moved = turned(vals[c], c - i)
+                    low = moved if low is None else jnp.where(quarter == c, moved, low)
+                high = None
+                for c in range(4):
+                    moved = turned(vals[4 + c % 2][8 * (c // 2) : 8 * (c // 2) + 8], c - i)
+                    high = moved if high is None else jnp.where(quarter[:8] == c, moved, high)
+                give[blk * 8 + 4 * g + i, 0:16] = low.astype(BF16)
+                give[blk * 8 + 4 * g + i, 16:24] = high.astype(BF16)
+
+        @pl.when(b > 0)
+        def _():
+            send_block(block_of(b + 7))
+
         return 0
 
-    lax.fori_loop(0, POINTS // 256, back, 0)
-
-    def pack(g, _):
-        cols = pl.ds(pl.multiple_of(g * 128, 128), 128)
-        vals = [spect[16 * c : 16 * c + 16, cols] for c in range(COMPS)]
-        for i in range(4):
-            near = None
-            for c in range(4):
-                moved = turned(vals[c], c - i)
-                near = moved if near is None else jnp.where(quarter == c, moved, near)
-            far = None
-            for c in range(4):
-                moved = turned(vals[4 + c % 2][8 * (c // 2) : 8 * (c // 2) + 8], c - i)
-                far = moved if far is None else jnp.where(quarter[:8] == c, moved, far)
-            give[4 * g + i, 0:16] = near.astype(BF16)
-            give[4 * g + i, 16:24] = far.astype(BF16)
-        return 0
-
-    lax.fori_loop(0, BLK // 4, pack, 0)
-
-    def send_second(i, _):
-        peer = lax.rem(here + i, BLK)
-        pltpu.make_async_remote_copy(
-            src_ref=give.at[peer], dst_ref=out_ref.at[here], send_sem=sems.at[2], recv_sem=sems.at[3],
-            device_id={"blk": peer}, device_id_type=MESH,
-        ).start()
-        return 0
-
-    lax.fori_loop(1, BLK, send_second, 0)
-    own = pltpu.make_async_copy(give.at[here], out_ref.at[here], sems.at[4])
+    lax.fori_loop(0, 8, spectra, 0)
+    send_block(block_of(7))
+    own = pltpu.make_async_copy(give.at[here], back.at[here], sems.at[4])
     own.start()
     own.wait()
+    load.wait()
     pltpu.make_async_remote_copy(
-        src_ref=give.at[0 : BLK - 1], dst_ref=out_ref.at[0 : BLK - 1], send_sem=sems.at[2], recv_sem=sems.at[3],
+        src_ref=give.at[0 : BLK - 1], dst_ref=back.at[0 : BLK - 1], send_sem=sems.at[2], recv_sem=sems.at[3],
         device_id={"blk": here}, device_id_type=MESH,
     ).wait()
 
-
-def run_longitude(order_map, shift, vis, msg):
-    whole = pl.BlockSpec(memory_space=pltpu.VMEM)
+    def fetch(d):
+        first, rest = back[d, 0:16].astype(F32), back[d, 16:24].astype(F32)
+        return first, jnp.concatenate([rest, pltpu.roll(rest, 64, 1)], axis=0)
+
+    for t in range(TILES):
+        w = lat_ref[3:4, pl.ds(128 * t, 128)]
+        north = [fetch(8 * t + b) for b in range(8)]
+        south = [fetch(BLK - 1 - 8 * t - b) for b in range(8)]
+        for h in range(2):
+            up = jnp.concatenate([v[h] for v in north], axis=0)
+            down = jnp.concatenate([v[h] for v in south], axis=0)
+            side[t, 0, pl.ds(128 * h, 128), :] = (up + down).T * w
+            side[t, 1, pl.ds(128 * h, 128), :] = (up - down).T * w
+
+    share = DEG // SHELLS
+    pos = lax.broadcasted_iota(jnp.int32, (16, DEG), 1)
+    pos_even = (pos & 1) == 0
+    tiny = lax.broadcasted_iota(jnp.int32, (16, 16), 1)
+
+    def near_copy(k, p):
+        return pltpu.make_async_remote_copy(
+            src_ref=part.at[k, p], dst_ref=near.at[k, p], send_sem=pair_sems.at[0, k, p], recv_sem=pair_sems.at[1, k, p],
+            device_id={"shell": partner}, device_id_type=MESH,
+        )
+
+    def far_copy(p):
+        return pltpu.make_async_remote_copy(
+            src_ref=pass_on.at[p], dst_ref=far.at[p], send_sem=pair_sems.at[2, 0, p], recv_sem=pair_sems.at[2, 1, p],
+            device_id={"shell": across}, device_id_type=MESH,
+        )
+
+    def forward(p):
+        near_copy(0, p).wait_recv()
+        pass_on[p] = (held[0, p] + near[0, p].astype(F32)).astype(BF16)
+        far_copy(p).start()
+
+    def analyse(p, _):
+        first = ord_ref[here * ORDERS + 2 * p]
+        odd_first = first & 1
+        e = jnp.where(odd_first == 0, first, DEG - 1 - first)
+        rows = jnp.concatenate(
+            [
+                jnp.concatenate([side[t, half, pl.ds(8 * par + p, 16, stride=16), :] for t in range(TILES)], axis=1)
+                for par in range(2)
+                for half in range(2)
+            ],
+            axis=0,
+        ).astype(BF16)
+        both = lax.dot_general(rows, tab[p], NT, preferred_element_type=F32)
+        final = lax.dot_general(rows[32:48], last_ref[...], NT, preferred_element_type=F32)
+        final = jnp.sum(jnp.where(tiny == p, final, 0.0), axis=1, keepdims=True)
+        ca = jnp.where(pos_even, both[0:16], both[16:32])
+        cb = jnp.where(pos_even, both[32:48], both[48:64])
+        ca = jnp.where(pos >= e, pltpu.roll(ca, e, 1), 0.0)
+        cb = jnp.where(pos >= DEG - 1 - e, pltpu.roll(cb, DEG - 1, 1), 0.0)
+        cb = jnp.where(pos == DEG - 1, final, cb)
+        keep = jnp.full((16, DEG), odd_first) == 0
+        pair = (jnp.where(keep, ca, cb), jnp.where(keep, cb, ca))
+        for k in range(2):
+            for c in range(COMPS):
+                out_ref[c, 0, 2 * p + k] = pair[k][2 * c : 2 * c + 2].astype(BF16)
+        scaled = jnp.concatenate([pair[0][0:12], pair[1][0:12]], axis=0) * rad_ref[0]
+        for layer_index in range(2):
+            for core_index in range(2):
+                piece = scaled[:, share * (2 * layer_index + core_index) : share * (2 * layer_index + core_index + 1)]
+                is_across = layer_index != layer
+                k = jnp.where(is_across, 0, 1)
+
+                @pl.when(core_index == core)
+                def _():
+                    held[k, p] = piece
+
+                @pl.when(core_index != core)
+                def _():
+                    part[k, p] = piece.astype(BF16)
+
+        near_copy(0, p).start()
+        near_copy(1, p).start()
+
+        @pl.when(p > 0)
+        def _():
+            forward(p - 1)
+
+        return 0
+
+    lax.fori_loop(0, PAIRS, analyse, 0)
+    forward(PAIRS - 1)
+
+    def finish(p, _):
+        near_copy(1, p).wait_recv()
+        total = held[1, p] + near[1, p].astype(F32)
+        far_copy(p).wait_recv()
+        total = total + far[p].astype(F32)
+        for k in range(2):
+            for c in range(COMPS):
+                sum_ref[c, 2 * p + k] = total[12 * k + 2 * c : 12 * k + 2 * c + 2]
+        near_copy(0, p).wait_send()
+        near_copy(1, p).wait_send()
+        far_copy(p).wait_send()
+        return 0
+
+    lax.fori_loop(0, PAIRS, finish, 0)
+
+
+def run_tail(order_map, rad, shift, vis, lat, last, msg, tab):
+    smem, vmem = pl.BlockSpec(memory_space=pltpu.SMEM), pl.BlockSpec(memory_space=pltpu.VMEM)
+    share = DEG // SHELLS
+    block = (PAIRS, 24, share)
     return pl.pallas_call(
-        longitude_kernel,
-        in_specs=[pl.BlockSpec(memory_space=pltpu.SMEM)] + [whole] * 3,
-        out_specs=pl.BlockSpec(memory_space=pl.ANY),
-        out_shape=jax.ShapeDtypeStruct((BLK, 24, 128), BF16),
+        tail_kernel,
+        in_specs=[smem, smem, vmem, vmem, vmem, vmem, vmem, pl.BlockSpec(memory_space=pl.ANY)],
+        out_specs=[vmem, vmem],
+        out_shape=[
+            jax.ShapeDtypeStruct((COMPS, 1, ORDERS, PARTS, DEG), BF16),
+            jax.ShapeDtypeStruct((COMPS, ORDERS, PARTS, share), F32),
+        ],
         scratch_shapes=[
+            pltpu.VMEM((PAIRS, DEG, HALF), BF16),
             pltpu.VMEM((POINTS, KH), BF16),
             pltpu.VMEM((192, POINTS), BF16),
             pltpu.VMEM((192, KH), BF16),
-            pltpu.VMEM((96, POINTS), F32),
             pltpu.VMEM((CYC, POINTS), F32),
             pltpu.VMEM((BLK, 24, 128), BF16),
             pltpu.VMEM((BLK, 24, 128), BF16),
-            pltpu.SemaphoreType.DMA((5,)),
+            pltpu.VMEM((BLK, 24, 128), BF16),
+            pltpu.VMEM((TILES, 2, 256, 128), F32),
+            pltpu.VMEM((2,) + block, BF16),
+            pltpu.VMEM((2,) + block, F32),
+            pltpu.VMEM((2,) + block, BF16),
+            pltpu.VMEM(block, BF16),
+            pltpu.VMEM(block, BF16),
+            pltpu.SemaphoreType.DMA((6,)),
+            pltpu.SemaphoreType.DMA((3, 2, PAIRS)),
         ],
         compiler_params=pltpu.CompilerParams(collective_id=0, has_side_effects=True),
-        name="longitude",
-    )(order_map, shift, vis, msg)
-
-
-def gather_kernel(part_ref, out_ref, near, total, give, far, sems):
-    here = lax.axis_index("shell")
-    layer, core = here // 2, lax.rem(here, 2)
-    partner, across = 2 * layer + 1 - core, 2 * (1 - layer) + core
-    barrier = pltpu.get_barrier_semaphore()
-    for peer in (partner, across):
-        pl.semaphore_signal(barrier, inc=1, device_id={"shell": peer}, device_id_type=MESH)
-    pl.semaphore_wait(barrier, 2)
-    first = []
-    for c in range(COMPS):
-        for k in range(2):
-            share = 2 * (1 - layer if k == 0 else layer) + 1 - core
-            copy = pltpu.make_async_remote_copy(
-                src_ref=part_ref.at[share, c], dst_ref=near.at[k, c], send_sem=sems.at[0, k, c], recv_sem=sems.at[1, k, c],
-                device_id={"shell": partner}, device_id_type=MESH,
-            )
-            copy.start()
-            first.append(copy)
-    second = []
-    for c in range(COMPS):
-        first[2 * c].wait_recv()
-        give[c] = (part_ref[across, c].astype(F32) + near[0, c].astype(F32)).astype(BF16)
-        copy = pltpu.make_async_remote_copy(
-            src_ref=give.at[c], dst_ref=far.at[c], send_sem=sems.at[2, 0, c], recv_sem=sems.at[2, 1, c],
-            device_id={"shell": across}, device_id_type=MESH,
-        )
-        copy.start()
-        second.append(copy)
-    for c in range(COMPS):
-        first[2 * c + 1].wait_recv()
-        total[c] = part_ref[here, c].astype(F32) + near[1, c].astype(F32)
-    for c in range(COMPS):
-        second[c].wait_recv()
-        out_ref[c] = total[c] + far[c].astype(F32)
-    for copy in first + second:
-        copy.wait_send()
-
-
-def run_gather(part):
-    whole = pl.BlockSpec(memory_space=pltpu.VMEM)
-    shape = (COMPS, ORDERS, PARTS, DEG // SHELLS)
-    return pl.pallas_call(
-        gather_kernel,
-        in_specs=[whole],
-        out_specs=whole,
-        out_shape=jax.ShapeDtypeStruct(shape, F32),
-        scratch_shapes=[
-            pltpu.VMEM((2,) + shape, BF16),
-            pltpu.VMEM(shape, F32),
-            pltpu.VMEM(shape, BF16),
-            pltpu.VMEM(shape, BF16),
-            pltpu.SemaphoreType.DMA((3, 2, COMPS)),
-        ],
-        compiler_params=pltpu.CompilerParams(collective_id=1, has_side_effects=True),
-        name="gather",
-    )(part)
-
-
-def analysis_kernel(ord_ref, rad_ref, lat_ref, tail_ref, tab_ref, msg_ref, out_ref, sum_ref, side):
-    p = pl.program_id(0)
-    base = lax.axis_index("blk") * ORDERS
-
-    @pl.when(p == 0)
-    def _():
-        def fetch(d):
-            near, far = msg_ref[d, 0:16].astype(F32), msg_ref[d, 16:24].astype(F32)
-            return near, jnp.concatenate([far, pltpu.roll(far, 64, 1)], axis=0)
-
-        for t in range(TILES):
-            w = lat_ref[3:4, pl.ds(128 * t, 128)]
-            north = [fetch(8 * t + b) for b in range(8)]
-            south = [fetch(BLK - 1 - 8 * t - b) for b in range(8)]
-            for h in range(2):
-                lanes = pl.ds(128 * h, 128)
-                up = jnp.concatenate([v[h] for v in north], axis=0)
-                down = jnp.concatenate([v[h] for v in south], axis=0)
-                side[t, 0, lanes, :] = (up + down).T * w
-                side[t, 1, lanes, :] = (up - down).T * w
-
-    first = ord_ref[base + 2 * p]
-    odd_first = first & 1
-    e = jnp.where(odd_first == 0, first, DEG - 1 - first)
-    left = jnp.concatenate(
-        [
-            jnp.concatenate([side[t, half, pl.ds(8 * par + p, 16, stride=16), :] for t in range(TILES)], axis=1)
-            for par in range(2)
-            for half in range(2)
-        ],
-        axis=0,
-    ).astype(BF16)
-    both = lax.dot_general(left, tab_ref[0], NT, preferred_element_type=F32)
-    final = lax.dot_general(left[32:48], tail_ref[...], NT, preferred_element_type=F32)
-    final = jnp.sum(jnp.where(lax.broadcasted_iota(jnp.int32, (16, 16), 1) == p, final, 0.0), axis=1, keepdims=True)
-    pos = lax.broadcasted_iota(jnp.int32, (16, DEG), 1)
-    pos_even = (pos & 1) == 0
-    ca = jnp.where(pos_even, both[0:16], both[16:32])
-    cb = jnp.where(pos_even, both[32:48], both[48:64])
-    ca = jnp.where(pos >= e, pltpu.roll(ca, e, 1), 0.0)
-    cb = jnp.where(pos >= DEG - 1 - e, pltpu.roll(cb, DEG - 1, 1), 0.0)
-    cb = jnp.where(pos == DEG - 1, final, cb)
-    share = DEG // SHELLS
-    for coef, slot in ((ca, 2 * p + odd_first), (cb, 2 * p + 1 - odd_first)):
-        scaled = coef * rad_ref[0]
-        for c in range(COMPS):
-            out_ref[c, 0, slot] = coef[2 * c : 2 * c + 2].astype(BF16)
-            for i in range(SHELLS):
-                sum_ref[i, c, slot] = scaled[2 * c : 2 * c + 2, i * share : (i + 1) * share].astype(BF16)
-
-
-def run_analysis(order_map, rad, lat, tail, tab, msg):
-    full = lambda shape: pl.BlockSpec(shape, lambda i: (0,) * len(shape))
-    shape = (COMPS, 1, ORDERS, PARTS, DEG)
-    split = (SHELLS, COMPS, ORDERS, PARTS, DEG // SHELLS)
-    return pl.pallas_call(
-        analysis_kernel,
-        grid=(PAIRS,),
-        in_specs=[
-            pl.BlockSpec(memory_space=pltpu.SMEM),
-            pl.BlockSpec(memory_space=pltpu.SMEM),
-            full((8, HALF)),
-            full((16, HALF)),
-            pl.BlockSpec((1, DEG, HALF), lambda i: (i, 0, 0)),
-            full((BLK, 24, 128)),
-        ],
-        out_specs=[full(shape), full(split)],
-        out_shape=[jax.ShapeDtypeStruct(shape, BF16), jax.ShapeDtypeStruct(split, BF16)],
-        scratch_shapes=[pltpu.VMEM((TILES, 2, 256, 128), F32)],
-        name="analysis",
-    )(order_map, rad, lat, tail, tab, msg)
+        name="tail",
+    )(order_map, rad, shift, vis, lat, last, msg, tab)
 
 
 def shift_table():
@@ -590,10 +592,8 @@
 def shards(strain_spec, order_map, viscosity, radial_weight):
     lat, g = latitude_constants()
     lat, g = jnp.asarray(lat), jnp.asarray(g)
-    tab, tail, msg = run_legendre(order_map, lat, g, strain_spec)
-    msg = run_longitude(order_map, jnp.asarray(shift_table()), viscosity, msg)
-    spec, part = run_analysis(order_map, radial_weight, lat, tail, tab, msg)
-    return spec, run_gather(part)
+    tab, last, msg = run_legendre(order_map, lat, g, strain_spec)
+    return run_tail(order_map, radial_weight, jnp.asarray(shift_table()), viscosity, lat, last, msg, tab)
 
 
 def solution(mesh):

time: 77.8 us -> 69.4 us (0.89)
  the two profiles are of different devices: /device:TPU:97 before, /device:TPU:32 now
where the time goes in v4:
time: 69.4 us
  Pallas kernels  64.5 us (93%)
  local copies, waits for them, and re-layouts  3.63 us (5%)
  between operations  1.29 us (2%)
    pallas_call x1, Pallas kernels, run_tail(): pl.pallas_call(tail_kernel, in_specs=[smem, smem, vmem, vmem, vmem, vmem,...  49.6 us
    pallas_call x1, Pallas kernels, run_legendre(): pl.pallas_call(legendre_kernel, grid=(STEPS,), in_specs=[pl.BlockSpec(mem...  14.9 us
    unnamed x2, local copies, waits for them, and re-layouts  3.63 us

profile of v4, /device:TPU:32, one launch (start us, length us, event | category | flops | bytes accessed | tf_op | source)
XLA Modules:
  0.0 69.4 jit_solution(7022859053915513109)
XLA Ops:
  1.3 14.9 %legendre.1 = (bf16[8,1024,512]{2,1,0:T(8,128)(2,1)}, bf16[16,512]{1,0:T(8,128)(2,1)}, bf16[64,24,128]{2,1,0:T(8,128)(2,1)}) custom-call(s32[1024]{0:T(1024)} %ord_ref.3, f32[8,512]{1,0:T(8,128)} %constant.6.clone.lat_ref, f32[1,1024]{1,0:T(1,128)} %constant.7.clone.g_ref, bf16[6,1,16,2,1024]{4,3,2,1,0:T(2,128)(2,1)} %spec_ref.1), custom_call_target="tpu_custom_call" | custom-call | tf_op jit(solution)/shard_map/legendre/pallas_call | solution.py:237
  16.1 49.6 %tail.1 = (bf16[6,1,16,2,1024]{4,3,2,1,0:T(2,128)(2,1)}, f32[6,16,2,256]{3,2,1,0:T(2,128)}) custom-call(s32[1024]{0:T(1024)} %ord_ref.3, f32[1]{0:T(128)S(6)} %copy.11.rad_ref, f32[2,1024]{1,0:T(2,128)} %constant.8.clone.shift_ref, f32[1,16,2048]{2,1,0:T(8,128)} %vis_ref.1, f32[8,512]{1,0:T(8,128)} %constant.6.clone.lat_ref, ...), custom_call_target="tpu_custom_call" | custom-call | tf_op jit(solution)/shard_map/tail/pallas_call | solution.py:554
  65.7 2.0 %copy.12 = bf16[6,1,16,2,1024]{4,3,2,1,0:T(2,128)(2,1)} copy(bf16[6,1,16,2,1024]{4,3,2,1,0:T(2,128)(2,1)} %get-tuple-element.10) | data formatting | bytes 786432
  67.8 1.6 %copy.13 = f32[6,16,2,256]{3,2,1,0:T(2,128)} copy(f32[6,16,2,256]{3,2,1,0:T(2,128)} %get-tuple-element.11) | data formatting | bytes 393216

commit v5 on v4

v5 whole, which is shorter than its diff:
```python
import math

import jax
import jax.numpy as jnp
import numpy as np
from jax import lax
from jax.experimental import pallas as pl
from jax.experimental.pallas import tpu as pltpu
from jax.sharding import PartitionSpec as P

F32 = jnp.float32
BF16 = jnp.bfloat16
COMPS = 6
PARTS = 2
ORDERS = 16
DEG = 1024
HALF = 512
BLK = 64
SHELLS = 4
CYC = 16
POINTS = 2048
KH = POINTS // 2
LB = 256
LSTRIDE = LB + 1
TILES = HALF // 128
PAIRS = 8
TURN = 16
TURNS = LB // TURN
WIDE = DEG + 128
BIG = 2.0**40
SMALL = 2.0**-40
NT = (((1,), (1,)), ((), ()))
MESH = pl.DeviceIdType.MESH


def latitude_constants():
    j = np.arange(HALF, dtype=np.float64)
    theta = np.pi * (2.0 * j + 1.0) / (4.0 * HALF)
    x = np.cos(theta)
    logsin = np.log2(np.sin(theta))
    hi = np.round(logsin * 512.0) / 512.0
    lo = logsin - hi
    k = np.arange(1, HALF + 1, dtype=np.float64)
    phase = np.outer(k, 2.0 * j + 1.0) % (4.0 * HALF)
    series = np.sum(np.cos(phase * np.pi / (2.0 * HALF)) / (4.0 * k * k - 1.0)[:, None], axis=0)
    weight = (2.0 / (2.0 * HALF)) * (1.0 - 2.0 * series)
    m = np.arange(DEG, dtype=np.float64)
    fac = np.concatenate([[0.0], np.cumsum(np.log2(1.0 - 0.5 / np.arange(1, DEG)))])
    g = 0.5 * np.log2((2.0 * m + 1.0) / (4.0 * np.pi)) + 0.5 * fac
    lat = np.stack([x, hi, lo, weight]).astype(np.float32)
    return np.concatenate([lat, np.zeros((4, HALF), np.float32)]), g.astype(np.float32)[None]


def power_of(e):
    return jnp.where(e < -126.0, 0.0, jnp.exp(jnp.maximum(e, -126.0) * math.log(2.0)))


def legendre_init(ord_ref, lat_ref, g_ref, base, ca, cab, ini, expo, ini2, expo2, mark, bca):
    sub8 = lax.broadcasted_iota(jnp.int32, (8, 128), 0)
    even = jnp.zeros((8, 128), jnp.int32)
    for p in range(PAIRS):
        first = ord_ref[base + 2 * p]
        even = jnp.where(sub8 == p, jnp.where((first & 1) == 0, first, DEG - 1 - first), even)
    ma = even.astype(F32)
    mb = (DEG - 1.0) - ma
    delta = (even & 7).astype(F32) + 1.0
    start = mb + delta
    mark[...] = start
    lane = lax.broadcasted_iota(jnp.int32, (8, 128), 1).astype(F32)
    for b in range(DEG // 128 + 1):
        t = lane + float(128 * b)
        second = t >= start
        m = jnp.where(second, mb, ma)
        l = jnp.where(second, t - delta, t + ma)
        up = (l > m) & (l < DEG - 0.5)
        a2 = (4.0 * l * l - 1.0) / jnp.where(up, (l - m) * (l + m), 1.0)
        a = jnp.where(up, jnp.sqrt(jnp.where(up, a2, 1.0)), 0.0)
        below = l - 1.0
        top = jnp.where(below > m, (below - m) * (below + m), 0.0)
        ab = a * jnp.sqrt(top / jnp.maximum(4.0 * below * below - 1.0, 1.0))
        for k in range(128 // TURN):
            ca[b * (128 // TURN) + k] = pltpu.roll(a, (128 - TURN * k) % 128, 1)
            cab[b * (128 // TURN) + k] = pltpu.roll(ab, (128 - TURN * k) % 128, 1)
    glane = lax.broadcasted_iota(jnp.int32, (8, DEG), 1).astype(F32)
    for m, first, power in ((ma, ini, expo), (mb, ini2, expo2)):
        gm = jnp.sum(jnp.where(glane == m[:, :1], g_ref[...], 0.0), axis=1, keepdims=True)
        for t in range(TILES):
            cols = pl.ds(128 * t, 128)
            mh = m * lat_ref[1:2, cols]
            whole = jnp.floor(mh)
            first[t] = jnp.exp(((mh - whole) + m * lat_ref[2:3, cols] + gm) * math.log(2.0))
            power[t] = whole
    for r in range(TURN):
        bca[r, 0] = jnp.broadcast_to(ca[0][:, r : r + 1], (8, 128))
        bca[r, 1] = jnp.broadcast_to(cab[0][:, r : r + 1], (8, 128))


def place_pairs(ord_ref, spec_ref, base, lhs):
    pos = lax.broadcasted_iota(jnp.int32, (16, WIDE), 1)
    pos_even = (pos & 1) == 0

    def place(p, _):
        first = ord_ref[base + 2 * p]
        odd_first = first & 1
        e = jnp.where(odd_first == 0, first, DEG - 1 - first)
        pads = [jnp.zeros((4, DEG), F32)]
        empty = jnp.zeros((16, WIDE - DEG), F32)
        da = jnp.concatenate([spec_ref[c, 0, 2 * p + odd_first].astype(F32) for c in range(COMPS)] + pads, axis=0)
        db = jnp.concatenate([spec_ref[c, 0, 2 * p + 1 - odd_first].astype(F32) for c in range(COMPS)] + pads, axis=0)
        da = da * jnp.where(e == 0, 1.0, 2.0)
        db = jnp.concatenate([db * 2.0, empty], axis=1)
        da = jnp.concatenate([pltpu.roll(da, jnp.where(e == 0, 0, DEG - e), 1), empty], axis=1)
        db = pltpu.roll(db, (e & 7) + 1, 1)
        da = jnp.where(pos < DEG - e, da, 0.0)
        db = jnp.where(pos >= DEG - e + (e & 7), db, 0.0)
        lhs[p, 0:16] = jnp.where(pos_even, da, 0.0).astype(BF16)
        lhs[p, 16:32] = jnp.where(pos_even, 0.0, da).astype(BF16)
        lhs[p, 32:48] = jnp.where(pos_even, db, 0.0).astype(BF16)
        lhs[p, 48:64] = jnp.where(pos_even, 0.0, db).astype(BF16)
        return 0

    lax.fori_loop(0, PAIRS, place, 0)


def legendre_synthesis(ord_ref, lat_ref, g_ref, spec_ref, base, tab, tail, msg, refs):
    ca, cab, prev, cur, expo, ini, ini2, expo2, mark, bca, bcb, ft, acc, lhs, ns = refs
    legendre_init(ord_ref, lat_ref, g_ref, base, ca, cab, ini, expo, ini2, expo2, mark, bca)
    place_pairs(ord_ref, spec_ref, base, lhs)
    for t in range(TILES):
        prev[t] = jnp.zeros((8, 128), F32)
        cur[t] = jnp.zeros((8, 128), F32)
    acc[...] = jnp.zeros_like(acc)

    def multiply(block, i):
        rows = pl.ds(i * LSTRIDE, LB)
        half_index = lax.rem(block, 2)
        span = pl.ds(pl.multiple_of(block * LB, LB), LB)
        left = lhs[i, :, span]
        for half in range(2):
            table = jnp.concatenate([ft[half_index, 2 * half, rows, :], ft[half_index, 2 * half + 1, rows, :]], axis=1)
            table = table.astype(BF16)
            tab[i, span, 256 * half : 256 * half + 256] = table
            acc[i, half] += jnp.dot(left, table, preferred_element_type=F32)

    def recur(block, i, turns, opening):
        half_index = lax.rem(block, 2)
        xs = [jnp.broadcast_to(lat_ref[0:1, pl.ds(128 * t, 128)], (8, 128)) for t in range(TILES)]
        ps, cs, scales = [prev[t] for t in range(TILES)], [cur[t] for t in range(TILES)], [None] * TILES
        es = [expo[t] for t in range(TILES)]
        for k in range(turns):
            use, make = (bca, bcb) if k == 0 else (bcb, bca)
            chunk = block * TURNS + 2 * i + k
            av, abv = ca[chunk + 1], cab[chunk + 1]
            for r in range(TURN):
                if r % 8 == 0:
                    now = jnp.full((8, 128), chunk * TURN + r).astype(F32)
                    hit = mark[...] == now
                    for t in range(TILES):
                        big = jnp.abs(cs[t]) > BIG
                        f = jnp.where(big, SMALL, 1.0)
                        es[t] = jnp.where(hit, expo2[t], jnp.where(big, es[t] + 40.0, es[t]))
                        scales[t] = power_of(es[t])
                        ps[t], cs[t] = ps[t] * f, cs[t] * f
                if turns == 2:
                    make[r, 0] = jnp.broadcast_to(av[:, r : r + 1], (8, 128))
                    make[r, 1] = jnp.broadcast_to(abv[:, r : r + 1], (8, 128))
                a, ab = use[r, 0], use[r, 1]
                for t in range(TILES):
                    new = (a * xs[t]) * cs[t] - ab * ps[t]
                    if r % 8 == 0:
                        new = jnp.where(hit, ini2[t], new)
                        if opening and r == 0 and k == 0:
                            new = jnp.where(now == 0.0, ini[t], new)
                    ps[t], cs[t] = cs[t], new
                    ft[half_index, t, pl.ds(2 * TURN * i + TURN * k + r, 8, stride=LSTRIDE), :] = new * scales[t]
        for t in range(TILES):
            prev[t], cur[t], expo[t] = ps[t], cs[t], es[t]

    def first_block(i, _):
        recur(0, i, 2, True)
        return 0

    def middle(n, _):
        block, i = n // PAIRS, lax.rem(n, PAIRS)
        multiply(block - 1, i)
        recur(block, i, 2, False)
        return 0

    lax.fori_loop(0, PAIRS, first_block, 0)
    lax.fori_loop(PAIRS, PAIRS * (DEG // LB), middle, 0)
    recur(DEG // LB, 0, 1, False)

    def last_block(i, _):
        multiply(DEG // LB - 1, i)
        rows = pl.ds(i * LSTRIDE, 16)
        table = jnp.concatenate([ft[0, t, rows, :] for t in range(TILES)], axis=1).astype(BF16)
        tail[i] = table
        extra = jnp.dot(lhs[i, 32:64, DEG:WIDE][:, 0:16], table, preferred_element_type=F32)
        for t in range(TILES):
            cols = slice(128 * (t % 2), 128 * (t % 2) + 128)
            part = acc[i, t // 2]
            for par in range(2):
                sym, anti = part[32 * par : 32 * par + 16, cols], part[32 * par + 16 : 32 * par + 32, cols]
                if par:
                    sym = sym + extra[0:16, 128 * t : 128 * t + 128]
                    anti = anti + extra[16:32, 128 * t : 128 * t + 128]
                ns[t, pl.ds(par * 8 + i, 16, stride=16), :] = sym + anti
                ns[TILES + t, pl.ds(par * 8 + i, 16, stride=16), :] = sym - anti
        return 0

    lax.fori_loop(0, PAIRS, last_block, 0)
    lane = lax.broadcasted_iota(jnp.int32, (8, 128), 1)
    for t in range(2 * TILES):
        near, far = ns[t, 0:128].T, ns[t, 128:256].T
        moved = pltpu.roll(far, 64, 1)
        for b in range(8):
            d = (t % TILES) * 8 + b
            dest = d if t < TILES else BLK - 1 - d
            msg[dest, 0:16] = near[16 * b : 16 * b + 16].astype(BF16)
            msg[dest, 16:24] = jnp.where(lane < 64, far[16 * b : 16 * b + 8], moved[16 * b + 8 : 16 * b + 16]).astype(BF16)


def turn(phase):
    t = phase * (1.0 / KH) - 1.0
    z = t * t
    c = jnp.full_like(z, 0.0)
    s = jnp.full_like(z, 0.0)
    for i in range(8, -1, -1):
        c = c * z + float((-1) ** (i + 1) * math.pi ** (2 * i) / math.factorial(2 * i))
        s = s * z + float((-1) ** (i + 1) * math.pi ** (2 * i + 1) / math.factorial(2 * i + 1))
    return c, s * t


def wrap(value):
    return value - POINTS * jnp.floor(value * (1.0 / POINTS))


def turned(value, quarters):
    return pltpu.roll(value, (32 * quarters) % 128, 1) if quarters % 4 else value


def whole_kernel(
    ord_ref, rad_ref, shift_ref, vis_ref, lat_ref, g_ref, spec_ref, out_ref, sum_ref,
    tab, last_ref, msg_ref, wave, left, pm, vis, got, give, back, side, part, held, near, pass_on, far, sems, pair_sems, *refs,
):
    here = lax.axis_index("blk")
    shell = lax.axis_index("shell")
    layer, core = shell // 2, lax.rem(shell, 2)
    partner, across = 2 * layer + 1 - core, 2 * (1 - layer) + core
    barrier = pltpu.get_barrier_semaphore()

    def greet(i, _):
        pl.semaphore_signal(barrier, inc=1, device_id={"blk": lax.rem(here + i, BLK)}, device_id_type=MESH)
        return 0

    lax.fori_loop(1, BLK, greet, 0)
    for peer in (partner, across):
        pl.semaphore_signal(barrier, inc=1, device_id={"shell": peer}, device_id_type=MESH)

    legendre_synthesis(ord_ref, lat_ref, g_ref, spec_ref, here * ORDERS, tab, last_ref, msg_ref, refs)
    pl.semaphore_wait(barrier, BLK + 1)

    def send_first(i, _):
        peer = lax.rem(here + i, BLK)
        pltpu.make_async_remote_copy(
            src_ref=msg_ref.at[peer], dst_ref=got.at[here], send_sem=sems.at[0], recv_sem=sems.at[1],
            device_id={"blk": peer}, device_id_type=MESH,
        ).start()
        return 0

    lax.fori_loop(1, BLK, send_first, 0)
    own = pltpu.make_async_copy(msg_ref.at[here], got.at[here], sems.at[4])
    own.start()

    lane = lax.broadcasted_iota(jnp.int32, (8, 128), 1).astype(F32)
    sub8 = lax.broadcasted_iota(jnp.int32, (8, 128), 0)
    sc, ss = [], []
    for u in range(KH // 128):
        sc.append(jnp.broadcast_to(shift_ref[0:1, pl.ds(128 * u, 128)], (8, 128)))
        ss.append(jnp.broadcast_to(shift_ref[1:2, pl.ds(128 * u, 128)], (8, 128)))

    def make(src, _):
        even = jnp.zeros((8, 128), jnp.int32)
        for p in range(PAIRS):
            first = ord_ref[src * ORDERS + 2 * p]
            even = jnp.where(sub8 == p, jnp.where((first & 1) == 0, first, DEG - 1 - first), even)
        m = even.astype(F32)
        c, s = turn(wrap(m * lane))
        gc, gs = turn(wrap(m * 128.0))
        for u in range(KH // 128):
            oc = sc[u] * c - ss[u] * s
            os = -(ss[u] * c + sc[u] * s)
            rows = pl.ds(pl.multiple_of(src * 32, 32), 32)
            wave[rows, pl.ds(128 * u, 128)] = jnp.concatenate([c, oc, -s, -os], axis=0).astype(BF16)
            c, s = c * gc - s * gs, s * gc + c * gs
        return 0

    lax.fori_loop(0, BLK, make, 0)
    for j in range(CYC):
        row = jnp.where(here >= BLK // 2, CYC - 1 - j, j)
        vis[j : j + 1, :] = vis_ref[0, pl.ds(row, 1), :]

    own.wait()
    pltpu.make_async_remote_copy(
        src_ref=msg_ref.at[0 : BLK - 1], dst_ref=got.at[0 : BLK - 1], send_sem=sems.at[0], recv_sem=sems.at[1],
        device_id={"blk": here}, device_id_type=MESH,
    ).wait()

    wide = lax.broadcasted_iota(jnp.int32, (16, 128), 1)
    even = ((wide // 8) % 2) == 0
    quarter = wide // 32
    for g in range(BLK // 4):
        pieces = [(got[4 * g + i, 0:16].astype(F32), got[4 * g + i, 16:24].astype(F32)) for i in range(4)]
        for c in range(COMPS):
            total = None
            for i in range(4):
                first, rest = pieces[i]
                moved = turned(first, i - c) if c < 4 else jnp.concatenate([turned(rest, i - c), turned(rest, i - c - 2)], axis=0)
                total = moved if total is None else jnp.where(quarter == i, moved, total)
            left[16 * c : 16 * c + 16, pl.ds(128 * g, 128)] = jnp.where(even, total, 0.0).astype(BF16)
            left[96 + 16 * c : 112 + 16 * c, pl.ds(128 * g, 128)] = jnp.where(even, 0.0, total).astype(BF16)

    for u in range(KH // 256):
        cols = pl.ds(256 * u, 256)
        field = jnp.dot(left[...], wave[:, cols], preferred_element_type=F32)
        low, high = vis[:, cols], vis[:, pl.ds(KH + 256 * u, 256)]
        for c in range(COMPS):
            e, o = field[16 * c : 16 * c + 16], field[96 + 16 * c : 112 + 16 * c]
            first, second = low * (e + o), high * (e - o)
            pm[16 * c : 16 * c + 16, cols] = (first + second).astype(BF16)
            pm[96 + 16 * c : 112 + 16 * c, cols] = (first - second).astype(BF16)

    lanes = lax.broadcasted_iota(jnp.int32, (96, 256), 1)
    pick = ((lanes // 8) % 2) == 0

    def send_block(blk):
        for i in range(8):
            peer = blk * 8 + i

            @pl.when(peer != here)
            def _():
                pltpu.make_async_remote_copy(
                    src_ref=give.at[peer], dst_ref=back.at[here], send_sem=sems.at[2], recv_sem=sems.at[3],
                    device_id={"blk": peer}, device_id_type=MESH,
                ).start()

    def block_of(b):
        return lax.rem(b + here // 8, 8)

    def spectra(b, _):
        blk = block_of(b)
        rows = pl.ds(pl.multiple_of(blk * 256, 256), 256)
        both = lax.dot_general(pm[...], wave[rows, :], NT, preferred_element_type=F32)
        spect = jnp.where(pick, both[:96], both[96:]) * (2.0 * math.pi / POINTS)
        for g in range(2):
            vals = [spect[16 * c : 16 * c + 16, 128 * g : 128 * g + 128] for c in range(COMPS)]
            for i in range(4):
                low = None
                for c in range(4):
                    moved = turned(vals[c], c - i)
                    low = moved if low is None else jnp.where(quarter == c, moved, low)
                high = None
                for c in range(4):
                    moved = turned(vals[4 + c % 2][8 * (c // 2) : 8 * (c // 2) + 8], c - i)
                    high = moved if high is None else jnp.where(quarter[:8] == c, moved, high)
                give[blk * 8 + 4 * g + i, 0:16] = low.astype(BF16)
                give[blk * 8 + 4 * g + i, 16:24] = high.astype(BF16)

        @pl.when(b > 0)
        def _():
            send_block(block_of(b + 7))

        return 0

    lax.fori_loop(0, 8, spectra, 0)
    send_block(block_of(7))
    own = pltpu.make_async_copy(give.at[here], back.at[here], sems.at[4])
    own.start()
    own.wait()
    pltpu.make_async_remote_copy(
        src_ref=give.at[0 : BLK - 1], dst_ref=back.at[0 : BLK - 1], send_sem=sems.at[2], recv_sem=sems.at[3],
        device_id={"blk": here}, device_id_type=MESH,
    ).wait()

    def fetch(d):
        first, rest = back[d, 0:16].astype(F32), back[d, 16:24].astype(F32)
        return first, jnp.concatenate([rest, pltpu.roll(rest, 64, 1)], axis=0)

    for t in range(TILES):
        w = lat_ref[3:4, pl.ds(128 * t, 128)]
        north = [fetch(8 * t + b) for b in range(8)]
        south = [fetch(BLK - 1 - 8 * t - b) for b in range(8)]
        for h in range(2):
            up = jnp.concatenate([v[h] for v in north], axis=0)
            down = jnp.concatenate([v[h] for v in south], axis=0)
            side[t, 0, pl.ds(128 * h, 128), :] = (up + down).T * w
            side[t, 1, pl.ds(128 * h, 128), :] = (up - down).T * w

    share = DEG // SHELLS
    pos = lax.broadcasted_iota(jnp.int32, (16, DEG), 1)
    pos_even = (pos & 1) == 0
    tiny_even = (lax.broadcasted_iota(jnp.int32, (16, 16), 1) & 1) == 0

    def near_copy(k, p):
        return pltpu.make_async_remote_copy(
            src_ref=part.at[k, p], dst_ref=near.at[k, p], send_sem=pair_sems.at[0, k, p], recv_sem=pair_sems.at[1, k, p],
            device_id={"shell": partner}, device_id_type=MESH,
        )

    def far_copy(p):
        return pltpu.make_async_remote_copy(
            src_ref=pass_on.at[p], dst_ref=far.at[p], send_sem=pair_sems.at[2, 0, p], recv_sem=pair_sems.at[2, 1, p],
            device_id={"shell": across}, device_id_type=MESH,
        )

    def forward(p):
        near_copy(0, p).wait_recv()
        pass_on[p] = (held[0, p] + near[0, p].astype(F32)).astype(BF16)
        far_copy(p).start()

    def analyse(p, _):
        first = ord_ref[here * ORDERS + 2 * p]
        odd_first = first & 1
        e = jnp.where(odd_first == 0, first, DEG - 1 - first)
        rows = jnp.concatenate(
            [
                jnp.concatenate([side[t, half, pl.ds(8 * par + p, 16, stride=16), :] for t in range(TILES)], axis=1)
                for par in range(2)
                for half in range(2)
            ],
            axis=0,
        ).astype(BF16)
        both = lax.dot_general(rows, tab[p], NT, preferred_element_type=F32)
        final = lax.dot_general(rows[32:64], last_ref[p], NT, preferred_element_type=F32)
        final = jnp.where(tiny_even, final[0:16], final[16:32])
        ca = jnp.where(pos_even, both[0:16], both[16:32])
        cb = jnp.where(pos_even, both[32:48], both[48:64])
        ca = jnp.where(pos >= e, pltpu.roll(ca, e, 1), 0.0)
        cb = jnp.concatenate([cb, final, jnp.zeros((16, WIDE - DEG - 16), F32)], axis=1)
        cb = pltpu.roll(cb, WIDE - 1 - (e & 7), 1)[:, 0:DEG]
        cb = jnp.where(pos >= DEG - 1 - e, cb, 0.0)
        keep = jnp.full((16, DEG), odd_first) == 0
        pair = (jnp.where(keep, ca, cb), jnp.where(keep, cb, ca))
        for k in range(2):
            for c in range(COMPS):
                out_ref[c, 0, 2 * p + k] = pair[k][2 * c : 2 * c + 2].astype(BF16)
        scaled = jnp.concatenate([pair[0][0:12], pair[1][0:12]], axis=0) * rad_ref[0]
        for layer_index in range(2):
            for core_index in range(2):
                piece = scaled[:, share * (2 * layer_index + core_index) : share * (2 * layer_index + core_index + 1)]
                is_across = layer_index != layer
                k = jnp.where(is_across, 0, 1)

                @pl.when(core_index == core)
                def _():
                    held[k, p] = piece

                @pl.when(core_index != core)
                def _():
                    part[k, p] = piece.astype(BF16)

        near_copy(0, p).start()
        near_copy(1, p).start()

        @pl.when(p > 0)
        def _():
            forward(p - 1)

        return 0

    lax.fori_loop(0, PAIRS, analyse, 0)
    forward(PAIRS - 1)

    def finish(p, _):
        near_copy(1, p).wait_recv()
        total = held[1, p] + near[1, p].astype(F32)
        far_copy(p).wait_recv()
        total = total + far[p].astype(F32)
        for k in range(2):
            for c in range(COMPS):
                sum_ref[c, 2 * p + k] = total[12 * k + 2 * c : 12 * k + 2 * c + 2]
        near_copy(0, p).wait_send()
        near_copy(1, p).wait_send()
        far_copy(p).wait_send()
        return 0

    lax.fori_loop(0, PAIRS, finish, 0)


def run_whole(order_map, rad, shift, vis, lat, g, spec):
    smem, vmem = pl.BlockSpec(memory_space=pltpu.SMEM), pl.BlockSpec(memory_space=pltpu.VMEM)
    share = DEG // SHELLS
    block = (PAIRS, 24, share)
    return pl.pallas_call(
        whole_kernel,
        in_specs=[smem, smem, vmem, vmem, vmem, vmem, vmem],
        out_specs=[vmem, vmem],
        out_shape=[
            jax.ShapeDtypeStruct((COMPS, 1, ORDERS, PARTS, DEG), BF16),
            jax.ShapeDtypeStruct((COMPS, ORDERS, PARTS, share), F32),
        ],
        scratch_shapes=[
            pltpu.VMEM((PAIRS, DEG, HALF), BF16),
            pltpu.VMEM((PAIRS, 16, HALF), BF16),
            pltpu.VMEM((BLK, 24, 128), BF16),
            pltpu.VMEM((POINTS, KH), BF16),
            pltpu.VMEM((192, POINTS), BF16),
            pltpu.VMEM((192, KH), BF16),
            pltpu.VMEM((CYC, POINTS), F32),
            pltpu.VMEM((BLK, 24, 128), BF16),
            pltpu.VMEM((BLK, 24, 128), BF16),
            pltpu.VMEM((BLK, 24, 128), BF16),
            pltpu.VMEM((TILES, 2, 256, 128), F32),
            pltpu.VMEM((2,) + block, BF16),
            pltpu.VMEM((2,) + block, F32),
            pltpu.VMEM((2,) + block, BF16),
            pltpu.VMEM(block, BF16),
            pltpu.VMEM(block, BF16),
            pltpu.SemaphoreType.DMA((5,)),
            pltpu.SemaphoreType.DMA((3, 2, PAIRS)),
            pltpu.VMEM(((DEG // 128 + 1) * (128 // TURN), 8, 128), F32),
            pltpu.VMEM(((DEG // 128 + 1) * (128 // TURN), 8, 128), F32),
            pltpu.VMEM((TILES, 8, 128), F32),
            pltpu.VMEM((TILES, 8, 128), F32),
            pltpu.VMEM((TILES, 8, 128), F32),
            pltpu.VMEM((TILES, 8, 128), F32),
            pltpu.VMEM((TILES, 8, 128), F32),
            pltpu.VMEM((TILES, 8, 128), F32),
            pltpu.VMEM((8, 128), F32),
            pltpu.VMEM((TURN, 2, 8, 128), F32),
            pltpu.VMEM((TURN, 2, 8, 128), F32),
            pltpu.VMEM((2, TILES, PAIRS * LSTRIDE + 8, 128), F32),
            pltpu.VMEM((PAIRS, 2, 64, 256), F32),
            pltpu.VMEM((PAIRS, 64, WIDE), BF16),
            pltpu.VMEM((2 * TILES, 256, 128), F32),
        ],
        compiler_params=pltpu.CompilerParams(collective_id=0, has_side_effects=True),
        name="whole",
    )(order_map, rad, shift, vis, lat, g, spec)


def shift_table():
    k = np.arange(KH, dtype=np.float64)
    ang = 2.0 * np.pi * k / POINTS
    sign = 1.0 - 2.0 * (k % 2)
    return np.stack([sign * np.cos(ang), sign * np.sin(ang)]).astype(np.float32)


def shards(strain_spec, order_map, viscosity, radial_weight):
    lat, g = latitude_constants()
    lat, g = jnp.asarray(lat), jnp.asarray(g)
    return run_whole(order_map, radial_weight, jnp.asarray(shift_table()), viscosity, lat, g, strain_spec)


def solution(mesh):
    return jax.shard_map(
        shards,
        mesh=mesh,
        in_specs=(P(None, "shell", "blk", None, None), P(), P("shell", "blk", None), P("shell")),
        out_specs=(P(None, "shell", "blk", None, None), P(None, "blk", None, "shell")),
        check_vma=False,
    )
```

time: 69.4 us -> 60 us (0.86)
  the two profiles are of different devices: /device:TPU:32 before, /device:TPU:97 now
where the time goes in v5:
time: 60 us; the launch traced here: 59.1 us
  Pallas kernels  55 us (92%)
  local copies, waits for them, and re-layouts  2.73 us (5%)
  between operations  1.29 us (2%)
    pallas_call x1, Pallas kernels, run_whole(): pl.pallas_call(whole_kernel, in_specs=[smem, smem, vmem, vmem, vmem, vmem...  55 us
    unnamed x4, local copies, waits for them, and re-layouts  2.73 us

profile of v5, /device:TPU:97, one launch (start us, length us, event | category | flops | bytes accessed | tf_op | source)
XLA Modules:
  0.0 59.1 jit_solution(17204474179897999638)
XLA Ops:
  1.3 55.0 %whole.1 = (bf16[6,1,16,2,1024]{4,3,2,1,0:T(2,128)(2,1)}, f32[6,16,2,256]{3,2,1,0:T(2,128)}) custom-call(s32[1024]{0:T(1024)} %ord_ref.1, f32[1]{0:T(128)S(6)} %copy.11.rad_ref, f32[2,1024]{1,0:T(2,128)} %constant.8.clone.shift_ref, f32[1,16,2048]{2,1,0:T(8,128)} %vis_ref.1, f32[8,512]{1,0:T(8,128)} %constant.6.clone.lat_ref, ...), custom_call_target="tpu_custom_call" | custom-call | tf_op jit(solution)/shard_map/whole/pallas_call | solution.py:494
  56.3 0.0 copy-start
  56.3 2.1 %copy.12 = bf16[6,1,16,2,1024]{4,3,2,1,0:T(2,128)(2,1)} copy(bf16[6,1,16,2,1024]{4,3,2,1,0:T(2,128)(2,1)} %get-tuple-element.4) | data formatting | bytes 786432
  58.4 0.0 copy-done
  58.4 0.7 %copy.13 = f32[6,16,2,256]{3,2,1,0:T(2,128)} copy(f32[6,16,2,256]{3,2,1,0:T(2,128)S(1)} %copy-done) | data formatting | bytes 393216
Async XLA Ops:
  56.3 2.1 %copy-start = (f32[6,16,2,256]{3,2,1,0:T(2,128)S(1)}, f32[6,16,2,256]{3,2,1,0:T(2,128)}, u32[]{:S(2)}) copy-start(f32[6,16,2,256]{3,2,1,0:T(2,128)} %get-tuple-element.5) | copy-start | bytes 589828

commit v6 on v5

--- a/solution.py
+++ b/solution.py
@@ -33,7 +33,7 @@
 MESH = pl.DeviceIdType.MESH
 
 
-def latitude_constants():
+def constants():
     j = np.arange(HALF, dtype=np.float64)
     theta = np.pi * (2.0 * j + 1.0) / (4.0 * HALF)
     x = np.cos(theta)
@@ -47,15 +47,21 @@
     m = np.arange(DEG, dtype=np.float64)
     fac = np.concatenate([[0.0], np.cumsum(np.log2(1.0 - 0.5 / np.arange(1, DEG)))])
     g = 0.5 * np.log2((2.0 * m + 1.0) / (4.0 * np.pi)) + 0.5 * fac
-    lat = np.stack([x, hi, lo, weight]).astype(np.float32)
-    return np.concatenate([lat, np.zeros((4, HALF), np.float32)]), g.astype(np.float32)[None]
+    k = np.arange(KH, dtype=np.float64)
+    sign = 1.0 - 2.0 * (k % 2)
+    table = np.zeros((8, KH), np.float32)
+    table[0:4, 0:HALF] = np.stack([x, hi, lo, weight])
+    table[4, 0:DEG] = g
+    table[5] = sign * np.cos(2.0 * np.pi * k / POINTS)
+    table[6] = sign * np.sin(2.0 * np.pi * k / POINTS)
+    return table
 
 
 def power_of(e):
     return jnp.where(e < -126.0, 0.0, jnp.exp(jnp.maximum(e, -126.0) * math.log(2.0)))
 
 
-def legendre_init(ord_ref, lat_ref, g_ref, base, ca, cab, ini, expo, ini2, expo2, mark, bca):
+def legendre_init(ord_ref, lat_ref, base, ca, cab, ini, expo, ini2, expo2, mark, bca):
     sub8 = lax.broadcasted_iota(jnp.int32, (8, 128), 0)
     even = jnp.zeros((8, 128), jnp.int32)
     for p in range(PAIRS):
@@ -83,7 +89,7 @@
             cab[b * (128 // TURN) + k] = pltpu.roll(ab, (128 - TURN * k) % 128, 1)
     glane = lax.broadcasted_iota(jnp.int32, (8, DEG), 1).astype(F32)
     for m, first, power in ((ma, ini, expo), (mb, ini2, expo2)):
-        gm = jnp.sum(jnp.where(glane == m[:, :1], g_ref[...], 0.0), axis=1, keepdims=True)
+        gm = jnp.sum(jnp.where(glane == m[:, :1], lat_ref[4:5, :], 0.0), axis=1, keepdims=True)
         for t in range(TILES):
             cols = pl.ds(128 * t, 128)
             mh = m * lat_ref[1:2, cols]
@@ -95,36 +101,47 @@
         bca[r, 1] = jnp.broadcast_to(cab[0][:, r : r + 1], (8, 128))
 
 
+def shift_left(pieces, amount):
+    lane = lax.broadcasted_iota(jnp.int32, (16, 128), 1)
+    turned_pieces = [pltpu.roll(piece, lax.rem(128 - amount, 128), 1) for piece in pieces]
+    return [jnp.where(lane < 128 - amount, a, b) for a, b in zip(turned_pieces[:-1], turned_pieces[1:])]
+
+
 def place_pairs(ord_ref, spec_ref, base, lhs):
-    pos = lax.broadcasted_iota(jnp.int32, (16, WIDE), 1)
+    pos = lax.broadcasted_iota(jnp.int32, (16, 128), 1)
     pos_even = (pos & 1) == 0
+    zero = jnp.zeros((16, 128), F32)
 
     def place(p, _):
         first = ord_ref[base + 2 * p]
         odd_first = first & 1
         e = jnp.where(odd_first == 0, first, DEG - 1 - first)
+        delta = (e & 7) + 1
         pads = [jnp.zeros((4, DEG), F32)]
-        empty = jnp.zeros((16, WIDE - DEG), F32)
         da = jnp.concatenate([spec_ref[c, 0, 2 * p + odd_first].astype(F32) for c in range(COMPS)] + pads, axis=0)
         db = jnp.concatenate([spec_ref[c, 0, 2 * p + 1 - odd_first].astype(F32) for c in range(COMPS)] + pads, axis=0)
-        da = da * jnp.where(e == 0, 1.0, 2.0)
-        db = jnp.concatenate([db * 2.0, empty], axis=1)
-        da = jnp.concatenate([pltpu.roll(da, jnp.where(e == 0, 0, DEG - e), 1), empty], axis=1)
-        db = pltpu.roll(db, (e & 7) + 1, 1)
-        da = jnp.where(pos < DEG - e, da, 0.0)
-        db = jnp.where(pos >= DEG - e + (e & 7), db, 0.0)
-        lhs[p, 0:16] = jnp.where(pos_even, da, 0.0).astype(BF16)
-        lhs[p, 16:32] = jnp.where(pos_even, 0.0, da).astype(BF16)
-        lhs[p, 32:48] = jnp.where(pos_even, db, 0.0).astype(BF16)
-        lhs[p, 48:64] = jnp.where(pos_even, 0.0, db).astype(BF16)
+        da = pltpu.roll(da * jnp.where(e == 0, 1.0, 2.0), jnp.where(e == 0, 0, DEG - e), 1)
+        db = db * 2.0
+        pieces = [zero] + [db[:, 128 * k : 128 * k + 128] for k in range(DEG // 128)] + [zero]
+        pieces = shift_left(pieces, 128 - delta)
+        for k in range(WIDE // 128):
+            cols = pl.ds(128 * k, 128)
+            a = jnp.where(pos < DEG - e - 128 * k, da[:, 128 * k : 128 * k + 128], 0.0) if k < DEG // 128 else zero
+            b = jnp.where(pos >= DEG - e + (e & 7) - 128 * k, pieces[k], 0.0)
+            lhs[p, 0:16, cols] = jnp.where(pos_even, a, 0.0).astype(BF16)
+            lhs[p, 16:32, cols] = jnp.where(pos_even, 0.0, a).astype(BF16)
+            lhs[p, 32:48, cols] = jnp.where(pos_even, b, 0.0).astype(BF16)
+            lhs[p, 48:64, cols] = jnp.where(pos_even, 0.0, b).astype(BF16)
         return 0
 
     lax.fori_loop(0, PAIRS, place, 0)
 
 
-def legendre_synthesis(ord_ref, lat_ref, g_ref, spec_ref, base, tab, tail, msg, refs):
+def legendre_synthesis(ord_ref, lat_ref, spec_ref, base, tab, tail, msg, loads, refs):
     ca, cab, prev, cur, expo, ini, ini2, expo2, mark, bca, bcb, ft, acc, lhs, ns = refs
-    legendre_init(ord_ref, lat_ref, g_ref, base, ca, cab, ini, expo, ini2, expo2, mark, bca)
+    loads[0].wait()
+    legendre_init(ord_ref, lat_ref, base, ca, cab, ini, expo, ini2, expo2, mark, bca)
+    loads[1].wait()
     place_pairs(ord_ref, spec_ref, base, lhs)
     for t in range(TILES):
         prev[t] = jnp.zeros((8, 128), F32)
@@ -240,25 +257,29 @@
 
 
 def whole_kernel(
-    ord_ref, rad_ref, shift_ref, vis_ref, lat_ref, g_ref, spec_ref, out_ref, sum_ref,
-    tab, last_ref, msg_ref, wave, left, pm, vis, got, give, back, side, part, held, near, pass_on, far, sems, pair_sems, *refs,
+    ord_ref, rad_ref, vis_hbm, lat_hbm, spec_hbm, out_ref, sum_ref,
+    lat_ref, spec_ref, vis_ref, tab, last_ref, msg_ref, wave, left, pm, vis, got, give, back, side, part, held, near, coefs, sems, pair_sems, *refs,
 ):
     here = lax.axis_index("blk")
     shell = lax.axis_index("shell")
-    layer, core = shell // 2, lax.rem(shell, 2)
-    partner, across = 2 * layer + 1 - core, 2 * (1 - layer) + core
+    loads = [
+        pltpu.make_async_copy(src, dst, sems.at[5 + i])
+        for i, (src, dst) in enumerate(((lat_hbm, lat_ref), (spec_hbm, spec_ref), (vis_hbm, vis_ref)))
+    ]
+    for load in loads:
+        load.start()
     barrier = pltpu.get_barrier_semaphore()
 
     def greet(i, _):
         pl.semaphore_signal(barrier, inc=1, device_id={"blk": lax.rem(here + i, BLK)}, device_id_type=MESH)
         return 0
 
-    lax.fori_loop(1, BLK, greet, 0)
-    for peer in (partner, across):
-        pl.semaphore_signal(barrier, inc=1, device_id={"shell": peer}, device_id_type=MESH)
-
-    legendre_synthesis(ord_ref, lat_ref, g_ref, spec_ref, here * ORDERS, tab, last_ref, msg_ref, refs)
-    pl.semaphore_wait(barrier, BLK + 1)
+    lax.fori_loop(1, BLK, greet, 0, unroll=7)
+    for i in range(1, SHELLS):
+        pl.semaphore_signal(barrier, inc=1, device_id={"shell": lax.rem(shell + i, SHELLS)}, device_id_type=MESH)
+
+    legendre_synthesis(ord_ref, lat_ref, spec_ref, here * ORDERS, tab, last_ref, msg_ref, loads, refs)
+    pl.semaphore_wait(barrier, BLK + SHELLS - 2)
 
     def send_first(i, _):
         peer = lax.rem(here + i, BLK)
@@ -268,7 +289,7 @@
         ).start()
         return 0
 
-    lax.fori_loop(1, BLK, send_first, 0)
+    lax.fori_loop(1, BLK, send_first, 0, unroll=7)
     own = pltpu.make_async_copy(msg_ref.at[here], got.at[here], sems.at[4])
     own.start()
 
@@ -276,8 +297,8 @@
     sub8 = lax.broadcasted_iota(jnp.int32, (8, 128), 0)
     sc, ss = [], []
     for u in range(KH // 128):
-        sc.append(jnp.broadcast_to(shift_ref[0:1, pl.ds(128 * u, 128)], (8, 128)))
-        ss.append(jnp.broadcast_to(shift_ref[1:2, pl.ds(128 * u, 128)], (8, 128)))
+        sc.append(jnp.broadcast_to(lat_ref[5:6, pl.ds(128 * u, 128)], (8, 128)))
+        ss.append(jnp.broadcast_to(lat_ref[6:7, pl.ds(128 * u, 128)], (8, 128)))
 
     def make(src, _):
         even = jnp.zeros((8, 128), jnp.int32)
@@ -295,7 +316,8 @@
             c, s = c * gc - s * gs, s * gc + c * gs
         return 0
 
-    lax.fori_loop(0, BLK, make, 0)
+    lax.fori_loop(0, BLK, make, 0, unroll=4)
+    loads[2].wait()
     for j in range(CYC):
         row = jnp.where(here >= BLK // 2, CYC - 1 - j, j)
         vis[j : j + 1, :] = vis_ref[0, pl.ds(row, 1), :]
@@ -347,7 +369,7 @@
     def block_of(b):
         return lax.rem(b + here // 8, 8)
 
-    def spectra(b, _):
+    def spectra(b):
         blk = block_of(b)
         rows = pl.ds(pl.multiple_of(blk * 256, 256), 256)
         both = lax.dot_general(pm[...], wave[rows, :], NT, preferred_element_type=F32)
@@ -366,13 +388,13 @@
                 give[blk * 8 + 4 * g + i, 0:16] = low.astype(BF16)
                 give[blk * 8 + 4 * g + i, 16:24] = high.astype(BF16)
 
-        @pl.when(b > 0)
-        def _():
-            send_block(block_of(b + 7))
-
-        return 0
-
-    lax.fori_loop(0, 8, spectra, 0)
+    def spectra_and_send(b, _):
+        send_block(block_of(b + 7))
+        spectra(b)
+        return 0
+
+    spectra(0)
+    lax.fori_loop(1, 8, spectra_and_send, 0)
     send_block(block_of(7))
     own = pltpu.make_async_copy(give.at[here], back.at[here], sems.at[4])
     own.start()
@@ -401,22 +423,13 @@
     pos_even = (pos & 1) == 0
     tiny_even = (lax.broadcasted_iota(jnp.int32, (16, 16), 1) & 1) == 0
 
-    def near_copy(k, p):
+    def share_copy(i, p):
+        peer = lax.rem(shell + i, SHELLS)
         return pltpu.make_async_remote_copy(
-            src_ref=part.at[k, p], dst_ref=near.at[k, p], send_sem=pair_sems.at[0, k, p], recv_sem=pair_sems.at[1, k, p],
-            device_id={"shell": partner}, device_id_type=MESH,
+            src_ref=part.at[p, peer], dst_ref=near.at[p, i - 1],
+            send_sem=pair_sems.at[0, i - 1, p], recv_sem=pair_sems.at[1, i - 1, p],
+            device_id={"shell": peer}, device_id_type=MESH,
         )
-
-    def far_copy(p):
-        return pltpu.make_async_remote_copy(
-            src_ref=pass_on.at[p], dst_ref=far.at[p], send_sem=pair_sems.at[2, 0, p], recv_sem=pair_sems.at[2, 1, p],
-            device_id={"shell": across}, device_id_type=MESH,
-        )
-
-    def forward(p):
-        near_copy(0, p).wait_recv()
-        pass_on[p] = (held[0, p] + near[0, p].astype(F32)).astype(BF16)
-        far_copy(p).start()
 
     def analyse(p, _):
         first = ord_ref[here * ORDERS + 2 * p]
@@ -436,70 +449,65 @@
         ca = jnp.where(pos_even, both[0:16], both[16:32])
         cb = jnp.where(pos_even, both[32:48], both[48:64])
         ca = jnp.where(pos >= e, pltpu.roll(ca, e, 1), 0.0)
-        cb = jnp.concatenate([cb, final, jnp.zeros((16, WIDE - DEG - 16), F32)], axis=1)
-        cb = pltpu.roll(cb, WIDE - 1 - (e & 7), 1)[:, 0:DEG]
+        final = jnp.concatenate([final, jnp.zeros((16, 112), F32)], axis=1)
+        pieces = [cb[:, 128 * k : 128 * k + 128] for k in range(DEG // 128)] + [final]
+        cb = jnp.concatenate(shift_left(pieces, (e & 7) + 1), axis=1)
         cb = jnp.where(pos >= DEG - 1 - e, cb, 0.0)
         keep = jnp.full((16, DEG), odd_first) == 0
         pair = (jnp.where(keep, ca, cb), jnp.where(keep, cb, ca))
+        both = jnp.concatenate([pair[0][0:12], pair[1][0:12]], axis=0)
+        coefs[p] = both
+        scaled = both * rad_ref[0]
+        for i in range(SHELLS):
+            piece = scaled[:, share * i : share * i + share]
+            part[p, i] = piece.astype(BF16)
+
+            @pl.when(shell == i)
+            def _():
+                held[p] = piece
+
+        for i in (2, 1, 3):
+            share_copy(i, p).start()
+        return 0
+
+    lax.fori_loop(0, PAIRS, analyse, 0)
+
+    def emit(p, _):
         for k in range(2):
             for c in range(COMPS):
-                out_ref[c, 0, 2 * p + k] = pair[k][2 * c : 2 * c + 2].astype(BF16)
-        scaled = jnp.concatenate([pair[0][0:12], pair[1][0:12]], axis=0) * rad_ref[0]
-        for layer_index in range(2):
-            for core_index in range(2):
-                piece = scaled[:, share * (2 * layer_index + core_index) : share * (2 * layer_index + core_index + 1)]
-                is_across = layer_index != layer
-                k = jnp.where(is_across, 0, 1)
-
-                @pl.when(core_index == core)
-                def _():
-                    held[k, p] = piece
-
-                @pl.when(core_index != core)
-                def _():
-                    part[k, p] = piece.astype(BF16)
-
-        near_copy(0, p).start()
-        near_copy(1, p).start()
-
-        @pl.when(p > 0)
-        def _():
-            forward(p - 1)
-
-        return 0
-
-    lax.fori_loop(0, PAIRS, analyse, 0)
-    forward(PAIRS - 1)
+                out_ref[c, 0, 2 * p + k] = coefs[p, 12 * k + 2 * c : 12 * k + 2 * c + 2].astype(BF16)
+        return 0
+
+    lax.fori_loop(0, PAIRS, emit, 0)
 
     def finish(p, _):
-        near_copy(1, p).wait_recv()
-        total = held[1, p] + near[1, p].astype(F32)
-        far_copy(p).wait_recv()
-        total = total + far[p].astype(F32)
+        for i in range(1, SHELLS):
+            share_copy(i, p).wait()
+        total = held[p] + near[p, 0].astype(F32) + near[p, 1].astype(F32) + near[p, 2].astype(F32)
         for k in range(2):
             for c in range(COMPS):
                 sum_ref[c, 2 * p + k] = total[12 * k + 2 * c : 12 * k + 2 * c + 2]
-        near_copy(0, p).wait_send()
-        near_copy(1, p).wait_send()
-        far_copy(p).wait_send()
         return 0
 
     lax.fori_loop(0, PAIRS, finish, 0)
 
 
-def run_whole(order_map, rad, shift, vis, lat, g, spec):
+def run_whole(order_map, rad, vis, lat, spec):
     smem, vmem = pl.BlockSpec(memory_space=pltpu.SMEM), pl.BlockSpec(memory_space=pltpu.VMEM)
+    hbm = pl.BlockSpec(memory_space=pltpu.HBM)
     share = DEG // SHELLS
-    block = (PAIRS, 24, share)
     return pl.pallas_call(
         whole_kernel,
-        in_specs=[smem, smem, vmem, vmem, vmem, vmem, vmem],
+        in_specs=[smem, smem, hbm, hbm, hbm],
         out_specs=[vmem, vmem],
         out_shape=[
             jax.ShapeDtypeStruct((COMPS, 1, ORDERS, PARTS, DEG), BF16),
             jax.ShapeDtypeStruct((COMPS, ORDERS, PARTS, share), F32),
         ],
         scratch_shapes=[
+            pltpu.VMEM((8, KH), F32),
+            pltpu.VMEM(spec.shape, BF16),
+            pltpu.VMEM(vis.shape, F32),
             pltpu.VMEM((PAIRS, DEG, HALF), BF16),
             pltpu.VMEM((PAIRS, 16, HALF), BF16),
             pltpu.VMEM((BLK, 24, 128), BF16),
@@ -511,13 +519,12 @@
             pltpu.VMEM((BLK, 24, 128), BF16),
             pltpu.VMEM((BLK, 24, 128), BF16),
             pltpu.VMEM((TILES, 2, 256, 128), F32),
-            pltpu.VMEM((2,) + block, BF16),
-            pltpu.VMEM((2,) + block, F32),
-            pltpu.VMEM((2,) + block, BF16),
-            pltpu.VMEM(block, BF16),
-            pltpu.VMEM(block, BF16),
-            pltpu.SemaphoreType.DMA((5,)),
-            pltpu.SemaphoreType.DMA((3, 2, PAIRS)),
+            pltpu.VMEM((PAIRS, SHELLS, 24, share), BF16),
+            pltpu.VMEM((PAIRS, 24, share), F32),
+            pltpu.VMEM((PAIRS, SHELLS - 1, 24, share), BF16),
+            pltpu.VMEM((PAIRS, 24, DEG), F32),
+            pltpu.SemaphoreType.DMA((8,)),
+            pltpu.SemaphoreType.DMA((2, SHELLS - 1, PAIRS)),
             pltpu.VMEM(((DEG // 128 + 1) * (128 // TURN), 8, 128), F32),
             pltpu.VMEM(((DEG // 128 + 1) * (128 // TURN), 8, 128), F32),
             pltpu.VMEM((TILES, 8, 128), F32),
@@ -534,22 +541,14 @@
             pltpu.VMEM((PAIRS, 64, WIDE), BF16),
             pltpu.VMEM((2 * TILES, 256, 128), F32),
         ],
-        compiler_params=pltpu.CompilerParams(collective_id=0, has_side_effects=True),
+        compiler_params=pltpu.CompilerParams(collective_id=0, has_side_effects=True, vmem_limit_bytes=48 * 2**20),
         name="whole",
-    )(order_map, rad, shift, vis, lat, g, spec)
-
-
-def shift_table():
-    k = np.arange(KH, dtype=np.float64)
-    ang = 2.0 * np.pi * k / POINTS
-    sign = 1.0 - 2.0 * (k % 2)
-    return np.stack([sign * np.cos(ang), sign * np.sin(ang)]).astype(np.float32)
+    )(order_map, rad, vis, lat, spec)
 
 
 def shards(strain_spec, order_map, viscosity, radial_weight):
-    lat, g = latitude_constants()
-    lat, g = jnp.asarray(lat), jnp.asarray(g)
-    return run_whole(order_map, radial_weight, jnp.asarray(shift_table()), viscosity, lat, g, strain_spec)
+    stay = lambda x: pltpu.with_memory_space_constraint(x, pltpu.HBM)
+    return run_whole(stay(order_map), radial_weight, stay(viscosity), stay(jnp.asarray(constants())), stay(strain_spec))
 
 
 def solution(mesh):

time: 60 us -> 56 us (0.933); the launches traced: 59.1 us -> 55.8 us
  Pallas kernels: 55 us -> 53.1 us
  local copies, waits for them, and re-layouts: 2.73 us -> 1.42 us
    pallas_call x1, Pallas kernels: 55 us -> 53.1 us  [run_whole(): pl.pallas_call(whole_kernel, in_specs=[smem, smem, hbm, hbm, hbm], out_sp...]
    unnamed x4 -> x2, local copies, waits for them, and re-layouts: 2.73 us -> 1.42 us
where the time goes in v6:
time: 56 us; the launch traced here: 55.8 us
  Pallas kernels  53.1 us (95%)
  local copies, waits for them, and re-layouts  1.42 us (3%)
  between operations  1.29 us (2%)
    pallas_call x1, Pallas kernels, run_whole(): pl.pallas_call(whole_kernel, in_specs=[smem, smem, hbm, hbm, hbm], out_sp...  53.1 us
    unnamed x2, local copies, waits for them, and re-layouts  1.42 us

profile of v6, /device:TPU:97, one launch (start us, length us, event | category | flops | bytes accessed | tf_op | source)
XLA Modules:
  0.0 55.8 jit_solution(8516377195264797760)
XLA Ops:
  1.3 53.1 %whole.1 = (bf16[6,1,16,2,1024]{4,3,2,1,0:T(2,128)(2,1)S(1)}, f32[6,16,2,256]{3,2,1,0:T(2,128)S(1)}) custom-call(s32[1024]{0:T(1024)} %ord_ref.1, f32[1]{0:T(128)S(6)} %copy.9.rad_ref, f32[1,16,2048]{2,1,0:T(8,128)} %vis_hbm.1, f32[8,1024]{1,0:T(8,128)} %constant.2.clone.lat_hbm, bf16[6,1,16,2,1024]{4,3,2,1,0:T(2,128)(2,1)} %spec_hbm.1), custom_call_target="tpu_custom_call" | custom-call | tf_op jit(solution)/shard_map/whole/pallas_call | solution.py:499
  54.4 0.7 %copy.10 = bf16[6,1,16,2,1024]{4,3,2,1,0:T(2,128)(2,1)} copy(bf16[6,1,16,2,1024]{4,3,2,1,0:T(2,128)(2,1)S(1)} %get-tuple-element.4) | data formatting | bytes 786432
  55.1 0.7 %copy.11 = f32[6,16,2,256]{3,2,1,0:T(2,128)} copy(f32[6,16,2,256]{3,2,1,0:T(2,128)S(1)} %get-tuple-element.5) | data formatting | bytes 393216

commit v7 on v6

--- a/solution.py
+++ b/solution.py
@@ -112,7 +112,7 @@
     pos_even = (pos & 1) == 0
     zero = jnp.zeros((16, 128), F32)
 
-    def place(p, _):
+    def place(p):
         first = ord_ref[base + 2 * p]
         odd_first = first & 1
         e = jnp.where(odd_first == 0, first, DEG - 1 - first)
@@ -132,9 +132,8 @@
             lhs[p, 16:32, cols] = jnp.where(pos_even, 0.0, a).astype(BF16)
             lhs[p, 32:48, cols] = jnp.where(pos_even, b, 0.0).astype(BF16)
             lhs[p, 48:64, cols] = jnp.where(pos_even, 0.0, b).astype(BF16)
-        return 0
-
-    lax.fori_loop(0, PAIRS, place, 0)
+
+    return place
 
 
 def legendre_synthesis(ord_ref, lat_ref, spec_ref, base, tab, tail, msg, loads, refs):
@@ -142,7 +141,7 @@
     loads[0].wait()
     legendre_init(ord_ref, lat_ref, base, ca, cab, ini, expo, ini2, expo2, mark, bca)
     loads[1].wait()
-    place_pairs(ord_ref, spec_ref, base, lhs)
+    place = place_pairs(ord_ref, spec_ref, base, lhs)
     for t in range(TILES):
         prev[t] = jnp.zeros((8, 128), F32)
         cur[t] = jnp.zeros((8, 128), F32)
@@ -194,6 +193,7 @@
             prev[t], cur[t], expo[t] = ps[t], cs[t], es[t]
 
     def first_block(i, _):
+        place(i)
         recur(0, i, 2, True)
         return 0
 

time: 56 us -> 55.4 us (0.989)
  Pallas kernels: 53.1 us -> 52.5 us
    pallas_call x1, Pallas kernels: 53.1 us -> 52.5 us  [run_whole(): pl.pallas_call(whole_kernel, in_specs=[smem, smem, hbm, hbm, hbm], out_sp...]
where the time goes in v7:
time: 55.4 us; the launch traced here: 55.2 us
  Pallas kernels  52.5 us (95%)
  local copies, waits for them, and re-layouts  1.42 us (3%)
  between operations  1.29 us (2%)
    pallas_call x1, Pallas kernels, run_whole(): pl.pallas_call(whole_kernel, in_specs=[smem, smem, hbm, hbm, hbm], out_sp...  52.5 us
    unnamed x2, local copies, waits for them, and re-layouts  1.42 us

profile of v7, /device:TPU:97, one launch (start us, length us, event | category | flops | bytes accessed | tf_op | source)
XLA Modules:
  0.0 55.2 jit_solution(5160469023277472271)
XLA Ops:
  1.3 52.5 %whole.1 = (bf16[6,1,16,2,1024]{4,3,2,1,0:T(2,128)(2,1)S(1)}, f32[6,16,2,256]{3,2,1,0:T(2,128)S(1)}) custom-call(s32[1024]{0:T(1024)} %ord_ref.1, f32[1]{0:T(128)S(6)} %copy.9.rad_ref, f32[1,16,2048]{2,1,0:T(8,128)} %vis_hbm.1, f32[8,1024]{1,0:T(8,128)} %constant.2.clone.lat_hbm, bf16[6,1,16,2,1024]{4,3,2,1,0:T(2,128)(2,1)} %spec_hbm.1), custom_call_target="tpu_custom_call" | custom-call | tf_op jit(solution)/shard_map/whole/pallas_call | solution.py:499
  53.8 0.7 %copy.10 = bf16[6,1,16,2,1024]{4,3,2,1,0:T(2,128)(2,1)} copy(bf16[6,1,16,2,1024]{4,3,2,1,0:T(2,128)(2,1)S(1)} %get-tuple-element.4) | data formatting | bytes 786432
  54.6 0.7 %copy.11 = f32[6,16,2,256]{3,2,1,0:T(2,128)} copy(f32[6,16,2,256]{3,2,1,0:T(2,128)S(1)} %get-tuple-element.5) | data formatting | bytes 393216
